TPU v7x, 128 devices: a whole 4x4x4 slice. The times are simulated.
128 devices in a mesh: scen: 32 (over x, z, core), pos: 4 (over y).
Axes of the slice: x: 4, y: 4, z: 4, core: 2. Of those that a mesh axis runs over, the one named last changes fastest.
Arguments:
- losses: bfloat16 [16384, 65536], P('scen', 'pos'), may hold values from -1 to 1
- book_sizes: int32 [1024], replicated, may hold values from 1 to 2048, 65536 in all
- owner_books: int32 [1024], replicated, may hold values from 0 to 1023, each once
Outputs:
- covariance: float32 [1024, 1024], P(('scen', 'pos'))
- contribution: float32 [1024], P(('scen', 'pos'))
Inputs may be any that keep to these rules, and one draw needn't show every extreme that they name: `book_sizes`: book sizes are between 1 and 2048 and sum to 65536. `owner_books`: each book appears exactly once.
All inputs are finite; a program needn't handle non-finite values.
Results may differ from a plain program's by a relative error of at most 0.0003.
Values sent between devices are 32-bit elements; how exact they have to be, the bound alone decides.
A program may use at most 64 MiB of HBM per device.

v0:
```python
import math

import jax
import jax.numpy as jnp
from jax import lax
from jax.sharding import Mesh
from jax.sharding import PartitionSpec as P

SCEN = ("scen_0", "scen_1", "scen_2")
SCEN_POS = ("scen_0", "scen_1", "scen_2", "pos")


def split_up(x, dim, peers):
    before, after = (x.shape[:dim], x.shape[dim + 1 :])
    return jnp.moveaxis(x.reshape(*before, peers, -1, *after), dim, 0)


def sum_at_owner(x, axis, dim):
    parts = split_up(x, dim, lax.axis_size(axis))
    arrived = lax.all_to_all(parts, axis, split_axis=0, concat_axis=0, tiled=True)
    return arrived.sum(axis=0)


def copy_for_each(x, axis):
    copies = jnp.broadcast_to(x, (lax.axis_size(axis), *x.shape))
    return lax.all_to_all(copies, axis, split_axis=0, concat_axis=0, tiled=True)


def of_everyone(x, axis):
    return copy_for_each(x, axis).sum(axis=0)


def laid_out(parts, dim):
    parts = jnp.moveaxis(parts, 0, dim)
    lengths = parts.shape
    return parts.reshape(*lengths[:dim], lengths[dim] * lengths[dim + 1], *lengths[dim + 2 :])


def gather_directly(x, axis, dim):
    parts = copy_for_each(x, axis)
    return laid_out(parts, dim)


def by_axis(x, axes):
    for axis in axes:
        x = lax.psum(x, axis)
    return x


def per_device(losses, book_sizes, owner_books):
    scen_count = lax.axis_size(SCEN)
    pos_count = lax.axis_size("pos")
    pos_index = lax.axis_index("pos")
    s_local, p_local = losses.shape
    book_count = book_sizes.shape[0]
    total_scen = s_local * scen_count
    per_dev = book_count // (scen_count * pos_count)
    start = jnp.cumsum(book_sizes) - book_sizes
    finish = start + book_sizes
    width = math.gcd(p_local, 2048)

    def add_block(step, total):
        offset = step * width
        rows = lax.dynamic_slice_in_dim(losses, offset, width, 1)
        place = pos_index * p_local + offset + jnp.arange(width, dtype=jnp.int32)
        member = (place[:, None] >= start[None, :]) & (place[:, None] < finish[None, :])
        return total + jnp.dot(
            rows, member.astype(jnp.bfloat16), preferred_element_type=jnp.float32
        )

    partial_value = lax.fori_loop(
        0, p_local // width, add_block, jnp.zeros((s_local, book_count), jnp.float32)
    )
    layout = owner_books.reshape(scen_count, pos_count, per_dev)
    order = layout.transpose(1, 0, 2).reshape(-1)
    arranged = jnp.take(partial_value, order, axis=1)
    own_pnl = sum_at_owner(arranged, "pos", 1)
    own_mean = of_everyone(jnp.sum(own_pnl, axis=0), SCEN) / total_scen
    own_centered = own_pnl - own_mean
    arranged_cov = (
        jnp.dot(
            own_centered.T,
            gather_directly(own_centered, "pos", 1),
            precision=lax.Precision.HIGHEST,
            preferred_element_type=jnp.float32,
        )
        / total_scen
    )
    inverse = (
        jnp.zeros((book_count,), jnp.int32).at[order].set(jnp.arange(book_count, dtype=jnp.int32))
    )
    restored = jnp.take(arranged_cov, inverse, axis=1)
    covariance = sum_at_owner(restored, SCEN, 0)
    row_total = jnp.sum(covariance, axis=1)
    portfolio_variance = by_axis(jnp.sum(row_total), SCEN_POS)
    contribution = row_total / jnp.sqrt(portfolio_variance)
    return (covariance, contribution)


def solution(mesh):
    split = Mesh(
        mesh.devices.reshape(4, 4, 2, mesh.shape["pos"]), ("scen_0", "scen_1", "scen_2", "pos")
    )
    in_specs = (P(SCEN, "pos"), P(), P())
    out_specs = (P(SCEN_POS, None), P(SCEN_POS))
    return jax.shard_map(
        per_device, mesh=split, in_specs=in_specs, out_specs=out_specs, check_vma=False
    )
```

profile of v0, /device:TPU:0, one launch (start us, length us, event | category | flops | bytes accessed | tf_op | source)
XLA Modules:
  0.0 190.2 jit_solution(7901304906873196729)
XLA Ops:
  0.6 0.8 reshape.95
  1.7 1.0 reduce-window.9
  2.9 0.8 fusion.18
  3.6 35.3 %while.16 = (s32[]{:T(128)}, f32[512,1024]{1,0:T(8,128)S(1)}, bf16[512,16384]{1,0:T(8,128)(2,1)}, s32[]{:T(128)}, s32[1024]{0:T(1024)S(1)}, /*index=5*/s32[1024]...) while((s32[]{:T(128)}, f32[512,1024]{1,0:T(8,128)S(1)}, bf16[512,16384]{1,0:T(8,128)(2,1)}, ...), condition=%wide.region_4.5_spmd.clone, body=%wide.region_3.4_spmd.clone.sunk | while | flops 2154825728 | bytes 6316209 | solution.py:71
  3.6 4.4 %select_add_fusion.2 = f32[512,1024]{1,0:T(8,128)S(1)} fusion(f32[512,1024]{1,0:T(8,128)S(1)} %get-tuple-element.240, s32[1024]{0:T(1024)S(1)} %get-tuple-element.254, s32[1024]{0:T(1024)S(1)} %get-tuple-element.253, s32[2048]{0:T(1024)S(1)} %iota_add_fusion.2, bf16[512,16384]{1,0:T(8,128)(2,1)} %get-tuple-element.251, s32[]{:T(128)S(6)} %select_n.59, ...), kind=kOutput, calls=%fused_computation.10.clone.1 | convolution fusion | flops 2154823680 | bytes 6307845 | tf_op jit(solution)/shard_map/while/body/eval_jaxpr/dot_general | solution.py:67
  8.0 4.4 %select_add_fusion.2 = f32[512,1024]{1,0:T(8,128)S(1)} fusion(f32[512,1024]{1,0:T(8,128)S(1)} %get-tuple-element.240, s32[1024]{0:T(1024)S(1)} %get-tuple-element.254, s32[1024]{0:T(1024)S(1)} %get-tuple-element.253, s32[2048]{0:T(1024)S(1)} %iota_add_fusion.2, bf16[512,16384]{1,0:T(8,128)(2,1)} %get-tuple-element.251, s32[]{:T(128)S(6)} %select_n.59, ...), kind=kOutput, calls=%fused_computation.10.clone.1 | convolution fusion | flops 2154823680 | bytes 6307845 | tf_op jit(solution)/shard_map/while/body/eval_jaxpr/dot_general | solution.py:67
  12.4 4.4 %select_add_fusion.2 = f32[512,1024]{1,0:T(8,128)S(1)} fusion(f32[512,1024]{1,0:T(8,128)S(1)} %get-tuple-element.240, s32[1024]{0:T(1024)S(1)} %get-tuple-element.254, s32[1024]{0:T(1024)S(1)} %get-tuple-element.253, s32[2048]{0:T(1024)S(1)} %iota_add_fusion.2, bf16[512,16384]{1,0:T(8,128)(2,1)} %get-tuple-element.251, s32[]{:T(128)S(6)} %select_n.59, ...), kind=kOutput, calls=%fused_computation.10.clone.1 | convolution fusion | flops 2154823680 | bytes 6307845 | tf_op jit(solution)/shard_map/while/body/eval_jaxpr/dot_general | solution.py:67
  16.9 4.4 %select_add_fusion.2 = f32[512,1024]{1,0:T(8,128)S(1)} fusion(f32[512,1024]{1,0:T(8,128)S(1)} %get-tuple-element.240, s32[1024]{0:T(1024)S(1)} %get-tuple-element.254, s32[1024]{0:T(1024)S(1)} %get-tuple-element.253, s32[2048]{0:T(1024)S(1)} %iota_add_fusion.2, bf16[512,16384]{1,0:T(8,128)(2,1)} %get-tuple-element.251, s32[]{:T(128)S(6)} %select_n.59, ...), kind=kOutput, calls=%fused_computation.10.clone.1 | convolution fusion | flops 2154823680 | bytes 6307845 | tf_op jit(solution)/shard_map/while/body/eval_jaxpr/dot_general | solution.py:67
  21.3 4.4 %select_add_fusion.2 = f32[512,1024]{1,0:T(8,128)S(1)} fusion(f32[512,1024]{1,0:T(8,128)S(1)} %get-tuple-element.240, s32[1024]{0:T(1024)S(1)} %get-tuple-element.254, s32[1024]{0:T(1024)S(1)} %get-tuple-element.253, s32[2048]{0:T(1024)S(1)} %iota_add_fusion.2, bf16[512,16384]{1,0:T(8,128)(2,1)} %get-tuple-element.251, s32[]{:T(128)S(6)} %select_n.59, ...), kind=kOutput, calls=%fused_computation.10.clone.1 | convolution fusion | flops 2154823680 | bytes 6307845 | tf_op jit(solution)/shard_map/while/body/eval_jaxpr/dot_general | solution.py:67
  25.7 4.4 %select_add_fusion.2 = f32[512,1024]{1,0:T(8,128)S(1)} fusion(f32[512,1024]{1,0:T(8,128)S(1)} %get-tuple-element.240, s32[1024]{0:T(1024)S(1)} %get-tuple-element.254, s32[1024]{0:T(1024)S(1)} %get-tuple-element.253, s32[2048]{0:T(1024)S(1)} %iota_add_fusion.2, bf16[512,16384]{1,0:T(8,128)(2,1)} %get-tuple-element.251, s32[]{:T(128)S(6)} %select_n.59, ...), kind=kOutput, calls=%fused_computation.10.clone.1 | convolution fusion | flops 2154823680 | bytes 6307845 | tf_op jit(solution)/shard_map/while/body/eval_jaxpr/dot_general | solution.py:67
  30.1 4.4 %select_add_fusion.2 = f32[512,1024]{1,0:T(8,128)S(1)} fusion(f32[512,1024]{1,0:T(8,128)S(1)} %get-tuple-element.240, s32[1024]{0:T(1024)S(1)} %get-tuple-element.254, s32[1024]{0:T(1024)S(1)} %get-tuple-element.253, s32[2048]{0:T(1024)S(1)} %iota_add_fusion.2, bf16[512,16384]{1,0:T(8,128)(2,1)} %get-tuple-element.251, s32[]{:T(128)S(6)} %select_n.59, ...), kind=kOutput, calls=%fused_computation.10.clone.1 | convolution fusion | flops 2154823680 | bytes 6307845 | tf_op jit(solution)/shard_map/while/body/eval_jaxpr/dot_general | solution.py:67
  34.6 4.4 %select_add_fusion.2 = f32[512,1024]{1,0:T(8,128)S(1)} fusion(f32[512,1024]{1,0:T(8,128)S(1)} %get-tuple-element.240, s32[1024]{0:T(1024)S(1)} %get-tuple-element.254, s32[1024]{0:T(1024)S(1)} %get-tuple-element.253, s32[2048]{0:T(1024)S(1)} %iota_add_fusion.2, bf16[512,16384]{1,0:T(8,128)(2,1)} %get-tuple-element.251, s32[]{:T(128)S(6)} %select_n.59, ...), kind=kOutput, calls=%fused_computation.10.clone.1 | convolution fusion | flops 2154823680 | bytes 6307845 | tf_op jit(solution)/shard_map/while/body/eval_jaxpr/dot_general | solution.py:67
  39.0 1.3 copy-done
  40.3 1.9 %copy.19 = f32[512,1024]{0,1:T(8,128)S(1)} copy(f32[512,1024]{1,0:T(8,128)} %copy-done) | data formatting | bytes 4194304 | tf_op jit(solution)/shard_map/while | solution.py:71
  42.3 4.9 %gather_fusion = f32[1024,512]{1,0:T(8,128)} fusion(f32[512,1024]{0,1:T(8,128)S(1)} %copy.19, s32[1024]{0:T(1024)S(1)} %broadcast_clamp_fusion), kind=kCustom, calls=%fused_computation | custom fusion | bytes 4198400 | tf_op jit(solution)/shard_map/jit(_take)/gather | solution.py:76
  47.2 1.8 select_bitcast_fusion
  49.0 30.7 %all_to_all.21 = f32[4,512,256]{1,2,0:T(8,128)S(1)} all-to-all(f32[4,512,256]{1,2,0:T(8,128)S(1)} %select_bitcast_fusion), channel_id=1, replica_groups=mesh['scen_0'=4,'scen_1'=4,'scen_2'=2,'pos'=4] {'pos'}, dimensions={0} | all-to-all | bytes 4194304 | tf_op jit(solution)/shard_map/all_to_all | solution.py:20
  80.0 15.4 %all_to_all.22 = f32[32,1,256]{2,1,0:T(1,128)S(1)} all-to-all(f32[32,1,256]{2,1,0:T(1,128)S(1)} %broadcast_in_dim.47), channel_id=1, replica_groups=mesh['scen_0'=4,'scen_1'=4,'scen_2'=2,'pos'=4] {'scen_0','scen_1','scen_2'}, dimensions={0} | all-to-all | bytes 65536 | tf_op jit(solution)/shard_map/all_to_all | solution.py:26
  95.5 1.6 broadcast_in_dim.48
  97.1 3.6 %all-to-all-start.2 = ((f32[4,512,256]{1,2,0:T(8,128)}), f32[4,512,256]{1,2,0:T(8,128)S(1)}, u32[]{:S(2)}, u32[]{:S(2)}) async-start(f32[4,512,256]{1,2,0:T(8,128)} %broadcast_in_dim.48), calls=%async_computation.2 | async-start | bytes 4194304 | tf_op jit(solution)/shard_map/all_to_all | solution.py:26
  100.8 4.3 %scatter_custom_fusion = s32[1024]{0:T(1024)S(1)} fusion(s32[1024]{0:T(1024)S(1)} %bitcast.24, s32[1024]{0:T(1024)S(1)} %iota.14, s32[]{:T(128)} %constant.79.clone.1), kind=kCustom, calls=%fused_computation.27 | custom fusion | bytes 4100 | tf_op jit(solution)/shard_map/scatter | solution.py:90
  105.1 22.5 %all-to-all-done.2 = f32[4,512,256]{1,2,0:T(8,128)S(1)} async-done(((f32[4,512,256]{1,2,0:T(8,128)}), f32[4,512,256]{1,2,0:T(8,128)S(1)}, u32[]{:S(2)}, u32[]{:S(2)}) %all-to-all-start.2) | async-done | bytes 2097184 | tf_op jit(solution)/shard_map/all_to_all | solution.py:26
  127.6 2.9 %convolution_multiply_fusion = f32[256,1024]{1,0:T(8,128)} fusion(f32[512,256]{0,1:T(8,128)S(1)} %broadcast_subtract_fusion, f32[512,1024]{0,1:T(8,128)S(1)} %bitcast.20), kind=kOutput, calls=%fused_computation.15 | convolution fusion | flops 1610874880 | bytes 3670016 | tf_op jit(solution)/shard_map/dot_general | solution.py:81
  130.5 1.6 copy.21
  132.1 3.5 %gather_fusion.1 = f32[1024,256]{1,0:T(8,128)S(1)} fusion(f32[256,1024]{0,1:T(8,128)S(1)} %copy.21, s32[1024]{0:T(1024)S(1)} %fusion.13), kind=kCustom, calls=%fused_computation.1 | custom fusion | bytes 2101248 | tf_op jit(solution)/shard_map/jit(_take)/gather | solution.py:92
  136.0 20.1 %all_to_all.23 = f32[32,8,1024]{2,1,0:T(8,128)S(1)} all-to-all(f32[32,8,1024]{2,1,0:T(8,128)S(1)} %bitcast_select_fusion), channel_id=1, replica_groups=mesh['scen_0'=4,'scen_1'=4,'scen_2'=2,'pos'=4] {'scen_0','scen_1','scen_2'}, dimensions={0} | all-to-all | bytes 2097152 | tf_op jit(solution)/shard_map/all_to_all | solution.py:20
  156.1 1.0 fusion.17
  157.1 9.9 %psum.28 = f32[]{:T(128)} all-reduce(f32[]{:T(128)} %get-tuple-element.175), channel_id=1, replica_groups=mesh['scen_0'=4,'scen_1'=4,'scen_2'=2,'pos'=4] {'scen_0'}, use_global_device_ids=true, to_apply=%region_11.12 | all-reduce | flops 1 | bytes 8 | tf_op jit(solution)/shard_map/psum | solution.py:46
  167.0 9.4 %psum.29 = f32[]{:T(128)} all-reduce(f32[]{:T(128)} %psum.28), channel_id=1, replica_groups=mesh['scen_0'=4,'scen_1'=4,'scen_2'=2,'pos'=4] {'scen_1'}, use_global_device_ids=true, to_apply=%region_12.13 | all-reduce | flops 1 | bytes 8 | tf_op jit(solution)/shard_map/psum | solution.py:46
  176.4 3.1 %psum.30 = f32[]{:T(128)} all-reduce(f32[]{:T(128)} %psum.29), channel_id=1, replica_groups=mesh['scen_0'=4,'scen_1'=4,'scen_2'=2,'pos'=4] {'scen_2'}, use_global_device_ids=true, to_apply=%region_13.14 | all-reduce | flops 1 | bytes 8 | tf_op jit(solution)/shard_map/psum | solution.py:46
  179.5 9.5 %psum.31 = f32[]{:T(128)} all-reduce(f32[]{:T(128)} %psum.30), channel_id=1, replica_groups=mesh['scen_0'=4,'scen_1'=4,'scen_2'=2,'pos'=4] {'pos'}, use_global_device_ids=true, to_apply=%region_14.15 | all-reduce | flops 1 | bytes 8 | tf_op jit(solution)/shard_map/psum | solution.py:46
  189.7 0.5 broadcast_divide_fusion
  (29 shorter events, 1.3 us)
Async XLA Ops:
  38.9 1.4 copy-start
  97.1 30.5 %all-to-all-start.2 = ((f32[4,512,256]{1,2,0:T(8,128)}), f32[4,512,256]{1,2,0:T(8,128)S(1)}, u32[]{:S(2)}, u32[]{:S(2)}) async-start(f32[4,512,256]{1,2,0:T(8,128)} %broadcast_in_dim.48), calls=%async_computation.2 | async-start | bytes 4194304 | tf_op jit(solution)/shard_map/all_to_all | solution.py:26
where the time goes:
time: 191 us; the launch traced here: 190 us
  blocking collectives  98.1 us (51%)
  matrix products  37.9 us (20%)
  waiting for transfers between devices  22.5 us (12%)
  local copies, waits for them, and re-layouts  20.7 us (11%)
  other arithmetic  5.63 us (3%)
  starting transfers between devices  3.61 us (2%)
    all_to_all x2, blocking collectives, sum_at_owner(): lax.all_to_all(parts, axis, split_axis=0, concat_axis=0, tiled=True)  50.8 us
    dot_general x8, matrix products, add_block(): jnp.dot(rows, member.astype(jnp.bfloat16), preferred_element_type=jnp.flo...  35 us
    psum x4, blocking collectives, by_axis(): x = lax.psum(x, axis)  31.9 us
    all_to_all x1, waiting for transfers between devices, copy_for_each(): return lax.all_to_all(copies, axis, split_axis=0, concat_axis=0, tiled=True)  22.5 us
    all_to_all x1, blocking collectives, copy_for_each(): return lax.all_to_all(copies, axis, split_axis=0, concat_axis=0, tiled=True)  15.4 us
    gather x1, local copies, waits for them, and re-layouts, per_device(): arranged = jnp.take(partial_value, order, axis=1)  4.89 us
    scatter x1, local copies, waits for them, and re-layouts, per_device(): jnp.zeros((book_count,), jnp.int32).at[order]  4.31 us
  transfers between devices with their start and end apart: 1, of which 1 were waited for; matrix products, arithmetic and copies ran while one was open for 2% of the time, Pallas kernels for 0%

commit v1 on v0

v1 whole, which is shorter than its diff:
```python
import functools

import jax
import jax.numpy as jnp
from jax import lax
from jax.experimental import pallas as pl
from jax.experimental.pallas import tpu as pltpu
from jax.sharding import Mesh
from jax.sharding import PartitionSpec as P

LANES = 128
TILE = 256
BLOCK = 4096
SHORT = 384
X, Z, C, Y = "scen_0", "scen_1", "scen_2", "pos"
SCEN = (X, Z, C)
SCEN_POS = (X, Z, C, Y)
COLOURS = (((X, 0), (Z, 0), (Y, 0)), ((Z, 1), (Y, 1), (X, 0)), ((Y, 2), (X, 0), (Z, 0)))


def segsum_body(lo_ref, hi_ref, start_ref, x_ref, out_ref, col):
    step = pl.program_id(0)
    width = x_ref.shape[1]

    @pl.when(step == 0)
    def _():
        out_ref[...] = jnp.zeros_like(out_ref)
        for b in range(0, col.shape[0], LANES):
            row = start_ref[:, b : b + LANES]
            col[b : b + LANES, :] = jnp.broadcast_to(row, (LANES, LANES)).T

    base = step * width
    lane = lax.broadcasted_iota(jnp.int32, (TILE, LANES), 1)

    def add_tile(t, carry):
        r0 = pl.multiple_of(t * TILE, TILE)
        begin = col[pl.ds(r0, TILE), :] - base
        end = col[pl.ds(r0 + 1, TILE), :] - base
        parts = []
        for l in range(0, width, LANES):
            place = lane + l
            inside = (place >= begin) & (place < end)
            parts.append(jnp.where(inside, 1.0, 0.0).astype(jnp.bfloat16))
        member = jnp.concatenate(parts, axis=1)
        sums = lax.dot_general(
            member, x_ref[...], (((1,), (1,)), ((), ())), preferred_element_type=jnp.float32
        )
        for c in range(out_ref.shape[0]):
            out_ref[c, pl.ds(r0, TILE), :] += sums[:, LANES * c : LANES * (c + 1)]
        return carry

    lax.fori_loop(lo_ref[step], hi_ref[step] + 1, add_tile, 0)


def segment_sums(losses, start, lo, hi, books):
    rows, places = losses.shape
    whole = lambda i, *_: (0, 0)
    return pl.pallas_call(
        segsum_body,
        out_shape=jax.ShapeDtypeStruct((rows // LANES, books, LANES), jnp.float32),
        grid_spec=pltpu.PrefetchScalarGridSpec(
            num_scalar_prefetch=2,
            grid=(places // BLOCK,),
            in_specs=[
                pl.BlockSpec(start.shape, whole),
                pl.BlockSpec((rows, BLOCK), lambda i, *_: (0, i)),
            ],
            out_specs=pl.BlockSpec((rows // LANES, books, LANES), lambda i, *_: (0, 0, 0)),
            scratch_shapes=[pltpu.VMEM((start.shape[1], LANES), jnp.int32)],
        ),
        name="segment_sums",
        compiler_params=pltpu.CompilerParams(
            dimension_semantics=("arbitrary",), vmem_limit_bytes=40 << 20
        ),
    )(lo, hi, start, losses)


def split(x):
    high = x.astype(jnp.bfloat16)
    return high, (x - high.astype(jnp.float32)).astype(jnp.bfloat16)


def to_column(row):
    return jnp.broadcast_to(row, (LANES, LANES)).T


def exchange_body(
    cap, total, offs, owner, xc, cov, con,
    land, vsum, vland, yvec, z, full0, full1, own, gram, land1, land2, land3, part1, part2,
    ysend, yrecv, vsend, vrecv, psend, precv, rsend, rrecv,
):
    at = {name: lax.axis_index(name) for name in SCEN_POS}
    size = {X: 4, Z: 4, C: 2, Y: 4}
    full = (full0, full1)
    books = full0.shape[0]

    def peer(name, p):
        return lax.rem(at[name] + p, size[name])

    barrier = pltpu.get_barrier_semaphore()
    count = 0
    for name in SCEN_POS:
        for p in range(1, size[name]):
            pl.semaphore_signal(
                barrier, inc=1, device_id={name: peer(name, p)}, device_id_type=pl.DeviceIdType.MESH
            )
            count += 1
    pl.semaphore_wait(barrier, count)

    def send(src, dst, s, r, name, p):
        copy = pltpu.make_async_remote_copy(
            src_ref=src,
            dst_ref=dst,
            send_sem=s,
            recv_sem=r,
            device_id={name: peer(name, p)},
            device_id_type=pl.DeviceIdType.MESH,
        )
        copy.start()
        return copy

    started = []
    chunks = []
    for p in (2, 1, 3):
        chunks.append(
            send(
                xc.at[peer(Y, p), pl.ds(0, cap), :], land.at[p - 1],
                ysend.at[p - 1], yrecv.at[p - 1], Y, p,
            )
        )

    for b in range(0, cap, LANES):
        rows = slice(b, b + LANES)
        block = (xc[0, rows, :] + xc[1, rows, :]) + (xc[2, rows, :] + xc[3, rows, :])
        vsum[0, :, rows] = block.T.reshape(LANES // 8, 8, LANES).sum(axis=0)
    slot = 0
    for stage, name in enumerate((X, Z, C)):
        copies = []
        for p in range(1, size[name]):
            copies.append(
                send(vsum.at[stage], vland.at[slot], vsend.at[slot], vrecv.at[slot], name, p)
            )
            slot += 1
        value = vsum[stage]
        for n, copy in enumerate(copies):
            copy.wait_recv()
            value = value + vland[slot - len(copies) + n]
        vsum[stage + 1] = value
        started += copies
    ycopies = []
    for p in range(1, 4):
        ycopies.append(send(vsum.at[3], yvec.at[p - 1], vsend.at[slot], vrecv.at[slot], Y, p))
        slot += 1
    started += ycopies

    zero = jnp.zeros((8, LANES), jnp.float32)

    def centre(p, values, sums):
        z[p, 0:8, :] = zero
        z[p, cap + 8 : cap + 16, :] = zero
        mean = sums.sum(axis=0, keepdims=True) / total
        for b in range(0, cap, LANES):
            z[p, 8 + b : 8 + b + LANES, :] = values[b : b + LANES, :] - to_column(
                mean[:, b : b + LANES]
            )

    centre(0, xc.at[at[Y]], vsum[3])
    for n, p in enumerate((2, 1, 3)):
        ycopies[p - 1].wait_recv()
        chunks[n].wait_recv()
        centre(p, land.at[p - 1], yvec[p - 1])
    started += chunks

    first = [offs[lax.rem(at[Y] + 4 - p, 4)] for p in range(4)]

    def put(t, carry):
        row = t * 8
        value = None
        for p in range(4):
            u = lax.min(lax.max(row - first[p] + 8, 0), cap + 8)
            got = z[p, pl.ds(u, 8), :]
            value = got if value is None else value + got
        full0[pl.ds(pl.multiple_of(row, 8), 8), :] = value
        return carry

    lax.fori_loop(0, books // 8, put, 0, unroll=8)
    pair = send(full0, full1, psend, precv, C, 1)
    started.append(pair)

    core = at[C]

    def gather(h):
        def some(g, carry):
            k0 = (g // 4) * 64 + core * 32 + lax.rem(g, 4) * 8
            for r in range(8):
                book = owner[k0 + r]
                own[h, pl.ds(g * 8 + r, 1), :] = full[h][pl.ds(book, 1), :]
            return carry

        lax.fori_loop(0, own.shape[1] // 8, some, 0, unroll=2)

    gather(0)
    pair.wait_recv()
    gather(1)

    sums = [full[h][...].reshape(books // 8, 8, LANES).sum(axis=0).sum(axis=0, keepdims=True) for h in (0, 1)]
    square = (sums[0] * sums[0] + sums[1] * sums[1]).sum(axis=1, keepdims=True)
    gram[:, :, :, :, books : books + LANES] = jnp.broadcast_to(square, (4, 4, 4, 8, LANES))

    a0h, a0l = split(own[0])
    a1h, a1l = split(own[1])
    left = jnp.concatenate([a0h, a1h, a0h, a1h, a0l, a1l], axis=1)
    for b in range(0, books, TILE):
        b0h, b0l = split(full0[b : b + TILE, :])
        b1h, b1l = split(full1[b : b + TILE, :])
        right = jnp.concatenate([b0h, b1h, b0l, b1l, b0h, b1h], axis=1)
        got = lax.dot_general(
            left, right, (((1,), (1,)), ((), ())), preferred_element_type=jnp.float32
        )
        gram[:, :, :, :, b : b + TILE] = got.reshape(4, 4, 4, 8, TILE)

    third = gram.shape[4] // 3

    def pick(ref, dim, index):
        return ref.at[(slice(None),) * dim + (index,)]

    def scatter(stage, colour, source, lands):
        name, dim = COLOURS[colour][stage]
        copies = []
        for p in (2, 1, 3):
            copies.append(
                (p, send(
                    pick(source, dim, peer(name, p)), lands.at[colour, p - 1],
                    rsend.at[stage, colour, p - 1], rrecv.at[stage, colour, p - 1], name, p,
                ))
            )
        return copies

    def reduce(stage, colour, source, lands, copies):
        name, dim = COLOURS[colour][stage]
        value = pick(source, dim, at[name])[...]
        for p, copy in copies:
            copy.wait_recv()
            value = value + lands[colour, p - 1]
            started.append(copy)
        return value

    sources = [gram.at[:, :, :, :, pl.ds(third * c, third)] for c in range(3)]
    flying = [scatter(0, c, sources[c], land1) for c in range(3)]
    for c in range(3):
        part1[c] = reduce(0, c, sources[c], land1, flying[c])
        flying[c] = scatter(1, c, part1.at[c], land2)
    for c in range(3):
        part2[c] = reduce(1, c, part1.at[c], land2, flying[c])
        flying[c] = scatter(2, c, part2.at[c], land3)
    done = [reduce(2, c, part2.at[c], land3, flying[c]) for c in range(3)]
    last = books - 2 * third
    cov[:, 0:third] = done[0] / total
    cov[:, third : 2 * third] = done[1] / total
    cov[:, 2 * third :] = done[2][:, :last] / total
    row = cov[...].sum(axis=1, keepdims=True)
    variance = done[2][:, last : last + 1] / total
    con[...] = jnp.broadcast_to(row / jnp.sqrt(variance), con.shape)
    for copy in started:
        copy.wait_send()


def exchange(xc, first, owner, cap, total, collective):
    books = xc.shape[1]
    f32 = jnp.float32
    third = (books + LANES) // 3
    rows = books // 128
    dma = pltpu.SemaphoreType.DMA
    return pl.pallas_call(
        functools.partial(exchange_body, cap, total),
        out_shape=(
            jax.ShapeDtypeStruct((rows, books), f32),
            jax.ShapeDtypeStruct((rows, LANES), f32),
        ),
        in_specs=[
            pl.BlockSpec(memory_space=pltpu.SMEM),
            pl.BlockSpec(memory_space=pltpu.SMEM),
            pl.BlockSpec(memory_space=pltpu.VMEM),
        ],
        out_specs=[pl.BlockSpec(memory_space=pltpu.VMEM)] * 2,
        scratch_shapes=[
            pltpu.VMEM((3, cap, LANES), f32),
            pltpu.VMEM((4, 8, cap), f32),
            pltpu.VMEM((7, 8, cap), f32),
            pltpu.VMEM((3, 8, cap), f32),
            pltpu.VMEM((4, cap + 16, LANES), f32),
            pltpu.VMEM((books, LANES), f32),
            pltpu.VMEM((books, LANES), f32),
            pltpu.VMEM((2, books // 2, LANES), f32),
            pltpu.VMEM((4, 4, 4, 8, books + LANES), f32),
            pltpu.VMEM((3, 3, 4, 4, 8, third), f32),
            pltpu.VMEM((3, 3, 4, 8, third), f32),
            pltpu.VMEM((3, 3, 8, third), f32),
            pltpu.VMEM((3, 4, 4, 8, third), f32),
            pltpu.VMEM((3, 4, 8, third), f32),
            dma((3,)), dma((3,)), dma((10,)), dma((10,)), dma, dma,
            dma((3, 3, 3)), dma((3, 3, 3)),
        ],
        name="exchange_%d" % cap,
        compiler_params=pltpu.CompilerParams(
            collective_id=collective, has_side_effects=True, vmem_limit_bytes=40 << 20
        ),
    )(first, owner, xc)


def per_device(losses, book_sizes, owner_books):
    rows, places = losses.shape
    books = book_sizes.shape[0]
    me = lax.axis_index(Y)
    total = rows * lax.axis_size(SCEN)
    finish = jnp.cumsum(book_sizes)

    def book_at(place):
        return jnp.sum((finish[None, :] <= place[:, None]).astype(jnp.int32), axis=1)

    blocks = jnp.arange(4, dtype=jnp.int32) * places
    first = book_at(blocks) // 8 * 8
    mine = jnp.take(first, me)
    beyond = jnp.full((books + LANES,), 1 << 24, jnp.int32)
    starts = jnp.concatenate([finish - book_sizes, beyond])
    start = lax.dynamic_slice(starts, (mine,), (books + LANES,)) - me * places
    ahead = me * places + BLOCK * jnp.arange(places // BLOCK, dtype=jnp.int32)
    lo = (book_at(ahead) - mine) // TILE
    hi = (book_at(ahead + (BLOCK - 1)) - mine) // TILE
    xc = segment_sums(losses, start.reshape(1, -1), lo, hi, books)
    cov, con = exchange(xc, first, owner_books, books, total, 1)
    return cov, con[:, 0]


def solution(mesh):
    grid = Mesh(mesh.devices.reshape(4, 4, 2, mesh.shape["pos"]), SCEN_POS)
    return jax.shard_map(
        per_device,
        mesh=grid,
        in_specs=(P(SCEN, Y), P(), P()),
        out_specs=(P(SCEN_POS, None), P(SCEN_POS)),
        check_vma=False,
    )
```

time: 191 us -> 74 us (0.39)
  blocking collectives: 98.1 us -> 0 us
  Pallas kernels: 0 us -> 68.1 us
  matrix products: 37.9 us -> 0 us
  waiting for transfers between devices: 22.5 us -> 0 us
  local copies, waits for them, and re-layouts: 20.7 us -> 2.03 us
  starting transfers between devices: 3.61 us -> 0 us
  other arithmetic: 5.63 us -> 2.11 us
    pallas_call x0 -> x2, Pallas kernels: none -> 68.1 us  [the longest x1 57.7 us: exchange(): pl.pallas_call(functools.partial(exchange_body, cap, total), out_shape=(j...]
    all_to_all x3 -> x0, blocking collectives: 66.2 us -> none  [the longest x2 50.8 us: sum_at_owner(): lax.all_to_all(parts, axis, split_axis=0, concat_axis=0, tiled=True)]
    dot_general x9 -> x0, matrix products: 37.9 us -> none  [the longest x8 35 us: add_block(): jnp.dot(rows, member.astype(jnp.bfloat16), preferred_element_type=jnp.flo...]
    psum x4 -> x0, blocking collectives: 31.9 us -> none  [by_axis(): x = lax.psum(x, axis)]
    all_to_all x1 -> x0, waiting for transfers between devices: 22.5 us -> none  [copy_for_each(): return lax.all_to_all(copies, axis, split_axis=0, concat_axis=0, tiled=True)]
    gather x3 -> x0, local copies, waits for them, and re-layouts: 8.69 us -> none  [the longest x1 4.89 us: per_device(): arranged = jnp.take(partial_value, order, axis=1)]
    scatter x1 -> x0, local copies, waits for them, and re-layouts: 4.31 us -> none  [per_device(): jnp.zeros((book_count,), jnp.int32).at[order]]
    all_to_all x1 -> x0, starting transfers between devices: 3.61 us -> none  [copy_for_each(): return lax.all_to_all(copies, axis, split_axis=0, concat_axis=0, tiled=True)]
  transfers between devices with their start and end apart: 1 -> 0, of which waited for: 1 -> 0; matrix products, arithmetic and copies ran while one was open for 2% -> 0% of each run, Pallas kernels for 0% -> 0%
where the time goes in v1:
time: 74 us; the launch traced here: 73.6 us
  Pallas kernels  68.1 us (92%)
  other arithmetic  2.11 us (3%)
  local copies, waits for them, and re-layouts  2.03 us (3%)
  between operations  1.36 us (2%)
    pallas_call x1, Pallas kernels, exchange(): pl.pallas_call(functools.partial(exchange_body, cap, total), out_shape=(j...  57.7 us
    pallas_call x1, Pallas kernels, segment_sums(): pl.pallas_call(segsum_body, out_shape=jax.ShapeDtypeStruct((rows // LANES...  10.4 us

profile of v1, /device:TPU:0, one launch (start us, length us, event | category | flops | bytes accessed | tf_op | source)
XLA Modules:
  0.0 73.6 jit_solution(3680188576823969724)
XLA Ops:
  0.6 0.0 copy-start
  0.7 1.0 %reduce-window.9 = s32[8,128]{1,0:T(8,128)S(1)} reduce-window(s32[8,128]{1,0:T(8,128)} %bitcast.6, s32[]{:T(128)} %constant.53.clone.1), window={size=1x128 pad=0_0x127_0}, to_apply=%region_0.0 | reduce-window | flops 130048 | bytes 8196 | tf_op jit(solution)/shard_map/reduce-window
  1.6 0.1 slice.10
  1.7 0.1 slice_reduce_fusion
  1.9 0.8 %fusion.2 = (s32[1024]{0:T(1024)S(1)}, s32[1024]{0:T(1024)S(1)}) fusion(s32[1024]{0:T(1024)} %param.4, s32[8,128]{1,0:T(8,128)S(1)} %reduce-window.9, s32[8]{0:T(128)S(1)} %slice_reduce_fusion), kind=kLoop, calls=%fused_computation.24 | loop fusion | flops 2048 | bytes 16416 | tf_op jit(solution)/shard_map/sub | solution.py:325
  2.6 0.2 convert_reduce_fusion
  2.9 0.6 dynamic-slice.2
  4.1 0.1 fusion
  4.2 10.4 %segment_sums.1.xc = f32[4,1024,128]{2,1,0:T(8,128)S(1)} custom-call(s32[4]{0:T(128)S(1)} %and_select_fusion.1.lo_ref, s32[4]{0:T(128)S(1)} %and_select_fusion.hi_ref, s32[1,1152]{1,0:T(1,128)S(1)} %reshape.48.start_ref, bf16[512,16384]{1,0:T(8,128)(2,1)} %x_ref.1), custom_call_target="tpu_custom_call" | custom-call | tf_op jit(solution)/shard_map/segment_sums/pallas_call | solution.py:58
  14.6 0.0 copy-done
  14.6 57.7 %exchange_1024.1 = (f32[8,1024]{1,0:T(8,128)S(1)}, f32[8,128]{1,0:T(8,128)S(1)}) custom-call(s32[4]{0:T(128)S(1)} %fusion.1.offs, s32[1024]{0:T(1024)S(1)} %copy-done, f32[4,1024,128]{2,1,0:T(8,128)S(1)} %segment_sums.1.xc), custom_call_target="tpu_custom_call" | custom-call | tf_op jit(solution)/shard_map/exchange_1024/pallas_call | solution.py:274
  72.3 0.6 slice_reduce_fusion.1
  72.9 0.6 copy.6
  (7 shorter events, 0.1 us)
Async XLA Ops:
  0.6 14.0 %copy-start = (s32[1024]{0:T(1024)S(1)}, s32[1024]{0:T(1024)}, u32[]{:S(2)}) copy-start(s32[1024]{0:T(1024)} %owner.1) | copy-start | bytes 12292

commit v2 on v1

--- a/solution.py
+++ b/solution.py
@@ -85,9 +85,9 @@
 
 
 def exchange_body(
-    cap, total, offs, owner, xc, cov, con,
-    land, vsum, vland, yvec, z, full0, full1, own, gram, land1, land2, land3, part1, part2,
-    ysend, yrecv, vsend, vrecv, psend, precv, rsend, rrecv,
+    cap, total, offs, owners, xc, cov, con,
+    owner, land, vsum, vland, yvec, z, full0, full1, own, gram, land1, land2, land3, part1, part2,
+    ysend, yrecv, vsend, vrecv, psend, precv, rsend, rrecv, osem,
 ):
     at = {name: lax.axis_index(name) for name in SCEN_POS}
     size = {X: 4, Z: 4, C: 2, Y: 4}
@@ -97,27 +97,29 @@
     def peer(name, p):
         return lax.rem(at[name] + p, size[name])
 
+    fetch = pltpu.make_async_copy(owners, owner, osem)
+    fetch.start()
+    others = [{name: peer(name, p)} for name in SCEN_POS for p in range(1, size[name])]
+    others += [{C: peer(C, 1), Y: peer(Y, p)} for p in range(1, size[Y])]
     barrier = pltpu.get_barrier_semaphore()
-    count = 0
-    for name in SCEN_POS:
-        for p in range(1, size[name]):
-            pl.semaphore_signal(
-                barrier, inc=1, device_id={name: peer(name, p)}, device_id_type=pl.DeviceIdType.MESH
-            )
-            count += 1
-    pl.semaphore_wait(barrier, count)
-
-    def send(src, dst, s, r, name, p):
+    for other in others:
+        pl.semaphore_signal(barrier, inc=1, device_id=other, device_id_type=pl.DeviceIdType.MESH)
+    pl.semaphore_wait(barrier, len(others))
+
+    def send_to(src, dst, s, r, device):
         copy = pltpu.make_async_remote_copy(
             src_ref=src,
             dst_ref=dst,
             send_sem=s,
             recv_sem=r,
-            device_id={name: peer(name, p)},
+            device_id=device,
             device_id_type=pl.DeviceIdType.MESH,
         )
         copy.start()
         return copy
+
+    def send(src, dst, s, r, name, p):
+        return send_to(src, dst, s, r, {name: peer(name, p)})
 
     started = []
     chunks = []
@@ -134,7 +136,7 @@
         block = (xc[0, rows, :] + xc[1, rows, :]) + (xc[2, rows, :] + xc[3, rows, :])
         vsum[0, :, rows] = block.T.reshape(LANES // 8, 8, LANES).sum(axis=0)
     slot = 0
-    for stage, name in enumerate((X, Z, C)):
+    for stage, name in enumerate((X, Z)):
         copies = []
         for p in range(1, size[name]):
             copies.append(
@@ -147,11 +149,16 @@
             value = value + vland[slot - len(copies) + n]
         vsum[stage + 1] = value
         started += copies
-    ycopies = []
-    for p in range(1, 4):
-        ycopies.append(send(vsum.at[3], yvec.at[p - 1], vsend.at[slot], vrecv.at[slot], Y, p))
-        slot += 1
-    started += ycopies
+    ycopies = {}
+    for p in (2, 1, 3, 0):
+        for d in (0, 1):
+            if p or d:
+                ycopies[d, p] = send_to(
+                    vsum.at[2], yvec.at[4 * d + p], vsend.at[slot], vrecv.at[slot],
+                    {C: peer(C, d), Y: peer(Y, p)},
+                )
+                slot += 1
+    started += ycopies.values()
 
     zero = jnp.zeros((8, LANES), jnp.float32)
 
@@ -164,11 +171,13 @@
                 mean[:, b : b + LANES]
             )
 
-    centre(0, xc.at[at[Y]], vsum[3])
-    for n, p in enumerate((2, 1, 3)):
-        ycopies[p - 1].wait_recv()
+    ycopies[1, 0].wait_recv()
+    centre(0, xc.at[at[Y]], vsum[2] + yvec[4])
+    for n, p in ((1, 1), (2, 3), (0, 2)):
+        ycopies[0, p].wait_recv()
+        ycopies[1, p].wait_recv()
         chunks[n].wait_recv()
-        centre(p, land.at[p - 1], yvec[p - 1])
+        centre(p, land.at[p - 1], yvec[p] + yvec[4 + p])
     started += chunks
 
     first = [offs[lax.rem(at[Y] + 4 - p, 4)] for p in range(4)]
@@ -199,6 +208,7 @@
 
         lax.fori_loop(0, own.shape[1] // 8, some, 0, unroll=2)
 
+    fetch.wait()
     gather(0)
     pair.wait_recv()
     gather(1)
@@ -279,15 +289,16 @@
         ),
         in_specs=[
             pl.BlockSpec(memory_space=pltpu.SMEM),
-            pl.BlockSpec(memory_space=pltpu.SMEM),
+            pl.BlockSpec(memory_space=pl.ANY),
             pl.BlockSpec(memory_space=pltpu.VMEM),
         ],
         out_specs=[pl.BlockSpec(memory_space=pltpu.VMEM)] * 2,
         scratch_shapes=[
+            pltpu.SMEM(owner.shape, jnp.int32),
             pltpu.VMEM((3, cap, LANES), f32),
-            pltpu.VMEM((4, 8, cap), f32),
-            pltpu.VMEM((7, 8, cap), f32),
             pltpu.VMEM((3, 8, cap), f32),
+            pltpu.VMEM((6, 8, cap), f32),
+            pltpu.VMEM((8, 8, cap), f32),
             pltpu.VMEM((4, cap + 16, LANES), f32),
             pltpu.VMEM((books, LANES), f32),
             pltpu.VMEM((books, LANES), f32),
@@ -298,8 +309,8 @@
             pltpu.VMEM((3, 3, 8, third), f32),
             pltpu.VMEM((3, 4, 4, 8, third), f32),
             pltpu.VMEM((3, 4, 8, third), f32),
-            dma((3,)), dma((3,)), dma((10,)), dma((10,)), dma, dma,
-            dma((3, 3, 3)), dma((3, 3, 3)),
+            dma((3,)), dma((3,)), dma((13,)), dma((13,)), dma, dma,
+            dma((3, 3, 3)), dma((3, 3, 3)), dma,
         ],
         name="exchange_%d" % cap,
         compiler_params=pltpu.CompilerParams(
@@ -328,7 +339,14 @@
     lo = (book_at(ahead) - mine) // TILE
     hi = (book_at(ahead + (BLOCK - 1)) - mine) // TILE
     xc = segment_sums(losses, start.reshape(1, -1), lo, hi, books)
-    cov, con = exchange(xc, first, owner_books, books, total, 1)
+    last = book_at(blocks + (places - 1))
+    fits = jnp.max(last - first) < SHORT
+    cov, con = lax.cond(
+        fits,
+        lambda *a: exchange(*a, SHORT, total, 1),
+        lambda *a: exchange(*a, books, total, 2),
+        xc, first, owner_books,
+    )
     return cov, con[:, 0]
 
 

time: 74 us -> 62.1 us (0.84)
  Pallas kernels: 68.1 us -> 55.1 us
    pallas_call x1, Pallas kernels: 57.7 us -> 45.8 us  [exchange(): pl.pallas_call(functools.partial(exchange_body, cap, total), out_shape=(j...]
    pallas_call x1, Pallas kernels: 10.4 us -> 9.32 us  [segment_sums(): pl.pallas_call(segsum_body, out_shape=jax.ShapeDtypeStruct((rows // LANES...]
where the time goes in v2:
time: 62.1 us; the launch traced here: 61.5 us
  Pallas kernels  55.1 us (89%)
  other arithmetic  2.74 us (4%)
  between operations  2.05 us (3%)
  local copies, waits for them, and re-layouts  1.61 us (3%)
    pallas_call x1, Pallas kernels, exchange(): pl.pallas_call(functools.partial(exchange_body, cap, total), out_shape=(j...  45.8 us
    pallas_call x1, Pallas kernels, segment_sums(): pl.pallas_call(segsum_body, out_shape=jax.ShapeDtypeStruct((rows // LANES...  9.32 us

profile of v2, /device:TPU:0, one launch (start us, length us, event | category | flops | bytes accessed | tf_op | source)
XLA Modules:
  0.0 61.5 jit_solution(14456680562078672057)
XLA Ops:
  0.6 0.0 copy-start
  0.7 1.0 %reduce-window.9 = s32[8,128]{1,0:T(8,128)S(1)} reduce-window(s32[8,128]{1,0:T(8,128)} %bitcast.6, s32[]{:T(128)} %constant.56.clone.1), window={size=1x128 pad=0_0x127_0}, to_apply=%region_0.0 | reduce-window | flops 130048 | bytes 8196 | tf_op jit(solution)/shard_map/reduce-window
  1.6 0.1 slice.14
  1.7 0.1 slice_reduce_fusion.2
  1.9 0.8 %fusion.2 = (s32[1024]{0:T(1024)S(1)}, s32[1024]{0:T(1024)S(1)}) fusion(s32[1024]{0:T(1024)} %param.6, s32[8,128]{1,0:T(8,128)S(1)} %reduce-window.9, s32[8]{0:T(128)S(1)} %slice_reduce_fusion.2), kind=kLoop, calls=%fused_computation.28 | loop fusion | flops 2048 | bytes 16416 | tf_op jit(solution)/shard_map/sub | solution.py:336
  2.6 0.2 convert_reduce_fusion
  2.8 0.6 %subtract_reduce_fusion = (s32[]{:T(128)}, s32[4]{0:T(128)S(1)}) fusion(s32[4]{0:T(128)S(1)} %get-tuple-element.48, s32[4]{0:T(128)S(1)} %get-tuple-element.46), kind=kLoop, calls=%fused_computation.23 | loop fusion | flops 71 | bytes 52 | tf_op jit(solution)/shard_map/reduce_max | solution.py:343
  4.1 0.7 %dynamic-slice.2 = s32[1]{0:T(128)} dynamic-slice(s32[4]{0:T(128)S(1)} %get-tuple-element.52, s32[]{:T(128)S(6)} %select_n.24), dynamic_slice_sizes={1} | dynamic-slice | bytes 12 | solution.py:334
  5.5 0.1 fusion
  5.6 9.3 %segment_sums.1 = f32[4,1024,128]{2,1,0:T(8,128)S(1)} custom-call(s32[4]{0:T(128)S(1)} %and_select_fusion.1.lo_ref, s32[4]{0:T(128)S(1)} %and_select_fusion.hi_ref, s32[1,1152]{1,0:T(1,128)S(1)} %reshape.51.start_ref, bf16[512,16384]{1,0:T(8,128)(2,1)} %x_ref.1), custom_call_target="tpu_custom_call" | custom-call | tf_op jit(solution)/shard_map/segment_sums/pallas_call | solution.py:58
  15.0 0.0 copy-done
  15.0 45.9 %conditional.1 = (f32[8,1024]{1,0:T(8,128)S(1)}, f32[8]{0:T(128)S(1)}) conditional(s32[]{:T(128)} %convert_element_type.17, (s32[4]{0:T(128)S(1)}, s32[1024]{0:T(1024)S(1)}, f32[4,1024,128]{2,1,0:T(8,128)S(1)}) %tuple.36, (s32[4]{0:T(128)S(1)}, s32[1024]{0:T(1024)S(1)}, f32[4,1024,128]{2,1,0:T(8,128)S(1)}) %tuple.37), branch_computations={%region_7.8_spmd, %region_8.9_spmd} | conditional | bytes 80 | solution.py:344
  15.0 45.8 %exchange_384.1 = (f32[8,1024]{1,0:T(8,128)S(1)}, f32[8,128]{1,0:T(8,128)S(1)}) custom-call(s32[4]{0:T(128)S(1)} %get-tuple-element.22.offs, s32[1024]{0:T(1024)S(1)} %get-tuple-element.33.owners, f32[4,1024,128]{2,1,0:T(8,128)S(1)} %get-tuple-element.24.xc), custom_call_target="tpu_custom_call" | custom-call | tf_op jit(solution)/shard_map/cond/branch_1_fun/exchange_384/pallas_call | solution.py:284
  60.8 0.1 slice_reduce_fusion.1
  60.9 0.0 copy-start.1
  60.9 0.6 %copy.14 = f32[8,1024]{1,0:T(8,128)} copy(f32[8,1024]{1,0:T(8,128)S(1)} %get-tuple-element.63) | data formatting | bytes 65536
  61.5 0.0 copy-done.1
  (6 shorter events, 0.1 us)
Async XLA Ops:
  0.6 14.3 %copy-start = (s32[1024]{0:T(1024)S(1)}, s32[1024]{0:T(1024)}, u32[]{:S(2)}) copy-start(s32[1024]{0:T(1024)} %param.7) | copy-start | bytes 12292
  60.9 0.6 %copy-start.1 = (f32[8]{0:T(128)}, f32[8]{0:T(128)S(1)}, u32[]{:S(2)}) copy-start(f32[8]{0:T(128)S(1)} %get-tuple-element.64) | copy-start | bytes 100

commit v3 on v2

v3 whole, which is shorter than its diff:
```python
import functools

import jax
import jax.numpy as jnp
from jax import lax
from jax.experimental import pallas as pl
from jax.experimental.pallas import tpu as pltpu
from jax.sharding import Mesh
from jax.sharding import PartitionSpec as P

LANES = 128
TILE = 256
SHORT = 384
X, Z, C, Y = "scen_0", "scen_1", "scen_2", "pos"
SCEN = (X, Z, C)
SCEN_POS = (X, Z, C, Y)
COLOURS = (((X, 0), (Z, 0), (Y, 0)), ((Z, 1), (Y, 1), (X, 0)), ((Y, 2), (X, 0), (Z, 0)))


def segsum_body(blocks, sizes_ref, x_hbm, out_ref, facts_ref, kept, col, sems):
    books = out_ref.shape[1]
    places = x_hbm.shape[1]
    me = lax.axis_index(Y)
    f32 = jnp.float32
    copies = []
    for n, (at, width) in enumerate(blocks):
        piece = pl.ds(at, width)
        copies.append(pltpu.make_async_copy(x_hbm.at[:, piece], kept.at[:, piece], sems.at[n]))
        copies[-1].start()

    exact = lax.Precision.HIGHEST
    sizes = sizes_ref[...].astype(f32)
    down = lax.broadcasted_iota(jnp.int32, (LANES, LANES), 0)
    across = lax.broadcasted_iota(jnp.int32, (LANES, LANES), 1)
    upper = jnp.where(down <= across, 1.0, 0.0).astype(f32)
    within = jnp.dot(sizes, upper, precision=exact, preferred_element_type=f32)
    before = [jnp.zeros((1, LANES), f32)]
    for k in range(books // LANES - 1):
        before.append(before[-1] + within[k : k + 1, LANES - 1 : LANES])
    start = within - sizes + jnp.concatenate(before, axis=0)
    for k in range(books // LANES):
        col[LANES * k : LANES * (k + 1), :] = to_column(start[k : k + 1, :]).astype(jnp.int32)
    col[books:, :] = jnp.full((col.shape[0] - books, LANES), 1 << 24, jnp.int32)

    lane = lax.broadcasted_iota(jnp.int32, (1, LANES), 1)
    place = jnp.zeros((1, LANES), jnp.int32)
    for n, (at, width) in enumerate(blocks):
        place = jnp.where(lane == n, me * places + at, place)
        place = jnp.where(lane == 16 + n, me * places + at + width - 1, place)
    for j in range(4):
        place = jnp.where(lane == 32 + j, j * places, place)
        place = jnp.where(lane == 48 + j, j * places + places - 1, place)
    count = jnp.zeros((8, LANES), jnp.int32)
    for b in range(0, books, 8):
        count = count + jnp.where(col[b : b + 8, :] <= place, 1, 0)
    facts = jnp.sum(count, axis=0, keepdims=True) - 1
    facts = jnp.where((lane >= 32) & (lane < 48), facts // 8 * 8, facts)

    def fact(i):
        return jnp.sum(jnp.where(lane == i, facts, 0).astype(f32)).astype(jnp.int32)

    longest = fact(48) - fact(32)
    for j in range(1, 4):
        longest = jnp.maximum(longest, fact(48 + j) - fact(32 + j))
    facts_ref[...] = jnp.where(lane == 64, longest, facts)
    mine = fact(32 + me)
    spans = [((fact(n) - mine) // TILE, (fact(16 + n) - mine) // TILE) for n in range(len(blocks))]
    out_ref[...] = jnp.zeros_like(out_ref)

    lanes = lax.broadcasted_iota(jnp.int32, (TILE, LANES), 1)
    for n, (at, width) in enumerate(blocks):
        base = me * places + at
        copies[n].wait()

        def add_tile(t, carry):
            r0 = pl.multiple_of(t * TILE, TILE)
            g0 = pl.multiple_of(mine + r0, 8)
            begin = col[pl.ds(g0, TILE), :] - base
            end = col[pl.ds(g0 + 1, TILE), :] - base
            parts = []
            for l in range(0, width, LANES):
                inside = (lanes + l >= begin) & (lanes + l < end)
                parts.append(jnp.where(inside, 1.0, 0.0).astype(jnp.bfloat16))
            sums = lax.dot_general(
                jnp.concatenate(parts, axis=1), kept[:, at : at + width],
                (((1,), (1,)), ((), ())), preferred_element_type=f32,
            )
            for c in range(out_ref.shape[0]):
                out_ref[c, pl.ds(r0, TILE), :] += sums[:, LANES * c : LANES * (c + 1)]
            return carry

        lax.fori_loop(spans[n][0], spans[n][1] + 1, add_tile, 0)


def segment_sums(losses, sizes):
    rows, places = losses.shape
    books = sizes.shape[0]
    widths = [places // 4] * 3 + [places // 8] * 2
    blocks = tuple((sum(widths[:n]), w) for n, w in enumerate(widths))
    return pl.pallas_call(
        functools.partial(segsum_body, blocks),
        out_shape=(
            jax.ShapeDtypeStruct((rows // LANES, books, LANES), jnp.float32),
            jax.ShapeDtypeStruct((1, LANES), jnp.int32),
        ),
        in_specs=[pl.BlockSpec(memory_space=pltpu.VMEM), pl.BlockSpec(memory_space=pl.ANY)],
        out_specs=[pl.BlockSpec(memory_space=pltpu.VMEM)] * 2,
        scratch_shapes=[
            pltpu.VMEM((rows, places), jnp.bfloat16),
            pltpu.VMEM((2 * books + TILE, LANES), jnp.int32),
            pltpu.SemaphoreType.DMA((len(blocks),)),
        ],
        name="segment_sums",
        compiler_params=pltpu.CompilerParams(vmem_limit_bytes=48 << 20),
    )(sizes.reshape(books // LANES, LANES), losses)


def split(x):
    high = x.astype(jnp.bfloat16)
    return high, (x - high.astype(jnp.float32)).astype(jnp.bfloat16)


def to_column(row):
    return jnp.broadcast_to(row, (LANES, LANES)).T


def exchange_body(
    cap, total, offs, owners, xc, cov, con,
    owner, land, vsum, vland, yvec, z, full0, full1, own, gram, land1, land2, land3, part1, part2,
    ysend, yrecv, vsend, vrecv, psend, precv, rsend, rrecv, osem,
):
    at = {name: lax.axis_index(name) for name in SCEN_POS}
    size = {X: 4, Z: 4, C: 2, Y: 4}
    full = (full0, full1)
    books = full0.shape[0]

    def peer(name, p):
        return lax.rem(at[name] + p, size[name])

    fetch = pltpu.make_async_copy(owners, owner, osem)
    fetch.start()
    others = [{name: peer(name, p)} for name in SCEN_POS for p in range(1, size[name])]
    others += [{C: peer(C, 1), Y: peer(Y, p)} for p in range(1, size[Y])]
    barrier = pltpu.get_barrier_semaphore()
    for other in others:
        pl.semaphore_signal(barrier, inc=1, device_id=other, device_id_type=pl.DeviceIdType.MESH)
    pl.semaphore_wait(barrier, len(others))

    def send_to(src, dst, s, r, device):
        copy = pltpu.make_async_remote_copy(
            src_ref=src,
            dst_ref=dst,
            send_sem=s,
            recv_sem=r,
            device_id=device,
            device_id_type=pl.DeviceIdType.MESH,
        )
        copy.start()
        return copy

    def send(src, dst, s, r, name, p):
        return send_to(src, dst, s, r, {name: peer(name, p)})

    started = []
    chunks = []
    for p in (2, 1, 3):
        chunks.append(
            send(
                xc.at[peer(Y, p), pl.ds(0, cap), :], land.at[p - 1],
                ysend.at[p - 1], yrecv.at[p - 1], Y, p,
            )
        )

    for b in range(0, cap, LANES):
        rows = slice(b, b + LANES)
        block = (xc[0, rows, :] + xc[1, rows, :]) + (xc[2, rows, :] + xc[3, rows, :])
        vsum[0, :, rows] = block.T.reshape(LANES // 8, 8, LANES).sum(axis=0)
    slot = 0
    for stage, name in enumerate((X, Z)):
        copies = []
        for p in range(1, size[name]):
            copies.append(
                send(vsum.at[stage], vland.at[slot], vsend.at[slot], vrecv.at[slot], name, p)
            )
            slot += 1
        value = vsum[stage]
        for n, copy in enumerate(copies):
            copy.wait_recv()
            value = value + vland[slot - len(copies) + n]
        vsum[stage + 1] = value
        started += copies
    ycopies = {}
    for p in (2, 1, 3, 0):
        for d in (0, 1):
            if p or d:
                ycopies[d, p] = send_to(
                    vsum.at[2], yvec.at[4 * d + p], vsend.at[slot], vrecv.at[slot],
                    {C: peer(C, d), Y: peer(Y, p)},
                )
                slot += 1
    started += ycopies.values()

    zero = jnp.zeros((8, LANES), jnp.float32)

    def centre(p, values, sums):
        z[p, 0:8, :] = zero
        z[p, cap + 8 : cap + 16, :] = zero
        mean = sums.sum(axis=0, keepdims=True) / total
        for b in range(0, cap, LANES):
            z[p, 8 + b : 8 + b + LANES, :] = values[b : b + LANES, :] - to_column(
                mean[:, b : b + LANES]
            )

    ycopies[1, 0].wait_recv()
    centre(0, xc.at[at[Y]], vsum[2] + yvec[4])
    for n, p in ((1, 1), (2, 3), (0, 2)):
        ycopies[0, p].wait_recv()
        ycopies[1, p].wait_recv()
        chunks[n].wait_recv()
        centre(p, land.at[p - 1], yvec[p] + yvec[4 + p])
    started += chunks

    first = [offs[0, 32 + lax.rem(at[Y] + 4 - p, 4)] for p in range(4)]

    def put(t, carry):
        row = t * 8
        value = None
        for p in range(4):
            u = lax.min(lax.max(row - first[p] + 8, 0), cap + 8)
            got = z[p, pl.ds(u, 8), :]
            value = got if value is None else value + got
        full0[pl.ds(pl.multiple_of(row, 8), 8), :] = value
        return carry

    lax.fori_loop(0, books // 8, put, 0, unroll=8)
    pair = send(full0, full1, psend, precv, C, 1)
    started.append(pair)

    core = at[C]

    def gather(h):
        def some(g, carry):
            k0 = (g // 4) * 64 + core * 32 + lax.rem(g, 4) * 8
            for r in range(8):
                book = owner[k0 + r]
                own[h, pl.ds(g * 8 + r, 1), :] = full[h][pl.ds(book, 1), :]
            return carry

        lax.fori_loop(0, own.shape[1] // 8, some, 0, unroll=2)

    fetch.wait()
    gather(0)
    pair.wait_recv()
    gather(1)

    sums = [full[h][...].reshape(books // 8, 8, LANES).sum(axis=0).sum(axis=0, keepdims=True) for h in (0, 1)]
    square = (sums[0] * sums[0] + sums[1] * sums[1]).sum(axis=1, keepdims=True)
    pieces = books // LANES + 1
    each = pieces // 3
    gram[pieces - 1] = jnp.broadcast_to(square, (4, 4, 4, 8, LANES))

    def pick(ref, dim, index):
        return ref.at[(slice(None),) * dim + (index,)]

    def scatter(stage, n, source, lands):
        name, dim = COLOURS[n // each][stage]
        copies = []
        for p in (2, 1, 3):
            copies.append(
                (p, send(
                    pick(source, dim, peer(name, p)), lands.at[n, p - 1],
                    rsend.at[stage, n, p - 1], rrecv.at[stage, n, p - 1], name, p,
                ))
            )
        return copies

    def reduce(stage, n, source, lands, copies):
        name, dim = COLOURS[n // each][stage]
        value = pick(source, dim, at[name])[...]
        for p, copy in copies:
            copy.wait_recv()
            value = value + lands[n, p - 1]
            started.append(copy)
        return value

    order = [each * c + q for q in range(each) for c in range(3)]
    flying = {}
    a0h, a0l = split(own[0])
    a1h, a1l = split(own[1])
    left = jnp.concatenate([a0h, a1h, a0h, a1h, a0l, a1l], axis=1)
    for n in order:
        if n < pieces - 1:
            rows = slice(LANES * n, LANES * (n + 1))
            b0h, b0l = split(full0[rows, :])
            b1h, b1l = split(full1[rows, :])
            right = jnp.concatenate([b0h, b1h, b0l, b1l, b0h, b1h], axis=1)
            got = lax.dot_general(
                left, right, (((1,), (1,)), ((), ())), preferred_element_type=jnp.float32
            )
            gram[n] = got.reshape(4, 4, 4, 8, LANES)
        flying[n] = scatter(0, n, gram.at[n], land1)
    for n in order:
        part1[n] = reduce(0, n, gram.at[n], land1, flying[n])
        flying[n] = scatter(1, n, part1.at[n], land2)
    for n in order:
        part2[n] = reduce(1, n, part1.at[n], land2, flying[n])
        flying[n] = scatter(2, n, part2.at[n], land3)
    done = {n: reduce(2, n, part2.at[n], land3, flying[n]) for n in order}
    row = None
    for n in range(pieces - 1):
        value = done[n] / total
        cov[:, LANES * n : LANES * (n + 1)] = value
        row = value if row is None else row + value
    variance = done[pieces - 1] / total
    con[...] = row.sum(axis=1, keepdims=True) / jnp.sqrt(variance)
    for copy in started:
        copy.wait_send()


def exchange(xc, facts, owner, cap, total, collective):
    books = xc.shape[1]
    f32 = jnp.float32
    pieces = books // LANES + 1
    rows = books // 128
    dma = pltpu.SemaphoreType.DMA
    return pl.pallas_call(
        functools.partial(exchange_body, cap, total),
        out_shape=(
            jax.ShapeDtypeStruct((rows, books), f32),
            jax.ShapeDtypeStruct((rows, LANES), f32),
        ),
        in_specs=[
            pl.BlockSpec(memory_space=pltpu.SMEM),
            pl.BlockSpec(memory_space=pl.ANY),
            pl.BlockSpec(memory_space=pltpu.VMEM),
        ],
        out_specs=[pl.BlockSpec(memory_space=pltpu.VMEM)] * 2,
        scratch_shapes=[
            pltpu.SMEM(owner.shape, jnp.int32),
            pltpu.VMEM((3, cap, LANES), f32),
            pltpu.VMEM((3, 8, cap), f32),
            pltpu.VMEM((6, 8, cap), f32),
            pltpu.VMEM((8, 8, cap), f32),
            pltpu.VMEM((4, cap + 16, LANES), f32),
            pltpu.VMEM((books, LANES), f32),
            pltpu.VMEM((books, LANES), f32),
            pltpu.VMEM((2, books // 2, LANES), f32),
            pltpu.VMEM((pieces, 4, 4, 4, 8, LANES), f32),
            pltpu.VMEM((pieces, 3, 4, 4, 8, LANES), f32),
            pltpu.VMEM((pieces, 3, 4, 8, LANES), f32),
            pltpu.VMEM((pieces, 3, 8, LANES), f32),
            pltpu.VMEM((pieces, 4, 4, 8, LANES), f32),
            pltpu.VMEM((pieces, 4, 8, LANES), f32),
            dma((3,)), dma((3,)), dma((13,)), dma((13,)), dma, dma,
            dma((3, pieces, 3)), dma((3, pieces, 3)), dma,
        ],
        name="exchange_%d" % cap,
        compiler_params=pltpu.CompilerParams(
            collective_id=collective, has_side_effects=True, vmem_limit_bytes=40 << 20
        ),
    )(facts, owner, xc)


def per_device(losses, book_sizes, owner_books):
    rows, places = losses.shape
    books = book_sizes.shape[0]
    total = rows * lax.axis_size(SCEN)
    xc, facts = segment_sums(losses, book_sizes)
    fits = facts[0, 64] < SHORT
    cov, con = lax.cond(
        fits,
        lambda *a: exchange(*a, SHORT, total, 1),
        lambda *a: exchange(*a, books, total, 2),
        xc, facts, owner_books,
    )
    return cov, con[:, 0]


def solution(mesh):
    grid = Mesh(mesh.devices.reshape(4, 4, 2, mesh.shape["pos"]), SCEN_POS)
    return jax.shard_map(
        per_device,
        mesh=grid,
        in_specs=(P(SCEN, Y), P(), P()),
        out_specs=(P(SCEN_POS, None), P(SCEN_POS)),
        check_vma=False,
    )
```

time: 62.1 us -> 57.5 us (0.926)
  other arithmetic: 2.74 us -> 0 us
  Pallas kernels: 55.1 us -> 53.6 us
  between operations: 2.05 us -> 1.31 us
    pallas_call x1, Pallas kernels: 45.8 us -> 44.6 us  [exchange(): pl.pallas_call(functools.partial(exchange_body, cap, total), out_shape=(j...]
    another operation x2 -> x0, other arithmetic: 0.99 us -> none
    sub x2 -> x0, other arithmetic: 0.84 us -> none  [the longest x1 0.76 us: per_device(): starts = jnp.concatenate([finish - book_sizes, beyond])]
    another operation x2 -> x0, local copies, waits for them, and re-layouts: 0.79 us -> none  [the longest x1 0.67 us: per_device(): mine = jnp.take(first, me)]
    unnamed x5 -> x7, local copies, waits for them, and re-layouts: 0.63 us -> 1.3 us
    reduce_max x1 -> x0, other arithmetic: 0.64 us -> none  [per_device(): fits = jnp.max(last - first) < SHORT]
where the time goes in v3:
time: 57.5 us; the launch traced here: 57.2 us
  Pallas kernels  53.6 us (93%)
  local copies, waits for them, and re-layouts  2 us (3%)
  between operations  1.31 us (2%)
    pallas_call x1, Pallas kernels, exchange(): pl.pallas_call(functools.partial(exchange_body, cap, total), out_shape=(j...  44.6 us
    pallas_call x1, Pallas kernels, segment_sums(): pl.pallas_call(functools.partial(segsum_body, blocks), out_shape=(jax.Sha...  9.01 us
    unnamed x7, local copies, waits for them, and re-layouts  1.3 us

profile of v3, /device:TPU:0, one launch (start us, length us, event | category | flops | bytes accessed | tf_op | source)
XLA Modules:
  0.0 57.2 jit_solution(3969099889051836668)
XLA Ops:
  0.6 0.0 copy-start
  0.6 0.7 %copy-done = s32[1024]{0:T(1024)S(1)} copy-done((s32[1024]{0:T(1024)S(1)}, s32[1024]{0:T(1024)}, u32[]{:S(2)}) %copy-start) | copy-done | bytes 4120
  1.3 0.0 copy-start.1
  1.3 9.0 %segment_sums.1 = (f32[4,1024,128]{2,1,0:T(8,128)S(1)}, s32[1,128]{1,0:T(1,128)S(1)}) custom-call(s32[8,128]{1,0:T(8,128)S(1)} %bitcast.2, bf16[512,16384]{1,0:T(8,128)(2,1)} %x_hbm.1), custom_call_target="tpu_custom_call" | custom-call | tf_op jit(solution)/shard_map/segment_sums/pallas_call | solution.py:100
  10.3 0.6 %slice.10 = s32[1,1]{1,0:T(1,128)} slice(s32[1,128]{1,0:T(1,128)S(1)} %get-tuple-element.31), slice={[0:1], [64:65]} | slice | bytes 8 | tf_op jit(solution)/shard_map/slice | solution.py:369
  11.6 0.0 copy-done.1
  11.6 44.9 %conditional.1 = (f32[8,1024]{1,0:T(8,128)S(1)}, f32[8]{0:T(128)S(1)}) conditional(s32[]{:T(128)} %bitcast.1, (s32[1,128]{1,0:T(1,128)S(1)}, s32[1024]{0:T(1024)S(1)}, f32[4,1024,128]{2,1,0:T(8,128)S(1)}) %tuple.24, (s32[1,128]{1,0:T(1,128)S(1)}, s32[1024]{0:T(1024)S(1)}, f32[4,1024,128]{2,1,0:T(8,128)S(1)}) %tuple.25), branch_computations={%region_0.0_spmd, %region_1.0_spmd} | conditional | bytes 80 | solution.py:370
  11.8 44.6 %exchange_384.1 = (f32[8,1024]{1,0:T(8,128)S(1)}, f32[8,128]{1,0:T(8,128)S(1)}) custom-call(s32[1,128]{1,0:T(1,128)S(1)} %get-tuple-element.22.offs, s32[1024]{0:T(1024)S(1)} %get-tuple-element.23.owners, f32[4,1024,128]{2,1,0:T(8,128)S(1)} %get-tuple-element.24.xc), custom_call_target="tpu_custom_call" | custom-call | tf_op jit(solution)/shard_map/cond/branch_1_fun/exchange_384/pallas_call | solution.py:326
  56.4 0.1 slice_reduce_fusion.1
  56.5 0.0 copy-start.2
  56.5 0.6 %copy.12 = f32[8,1024]{1,0:T(8,128)} copy(f32[8,1024]{1,0:T(8,128)S(1)} %get-tuple-element.40) | data formatting | bytes 65536
  57.2 0.0 copy-done.2
Async XLA Ops:
  0.6 0.7 %copy-start = (s32[1024]{0:T(1024)S(1)}, s32[1024]{0:T(1024)}, u32[]{:S(2)}) copy-start(s32[1024]{0:T(1024)} %param.6) | copy-start | bytes 12292
  1.3 10.3 %copy-start.1 = (s32[1024]{0:T(1024)S(1)}, s32[1024]{0:T(1024)}, u32[]{:S(2)}) copy-start(s32[1024]{0:T(1024)} %param.7) | copy-start | bytes 12292
  56.5 0.6 %copy-start.2 = (f32[8]{0:T(128)}, f32[8]{0:T(128)S(1)}, u32[]{:S(2)}) copy-start(f32[8]{0:T(128)S(1)} %get-tuple-element.41) | copy-start | bytes 100

commit v4 on v3

--- a/solution.py
+++ b/solution.py
@@ -11,10 +11,40 @@
 LANES = 128
 TILE = 256
 SHORT = 384
+WINDOW = 128
+PAD = 32
+GROUPS = ((0, 1), (1, 3), (3, 4))
 X, Z, C, Y = "scen_0", "scen_1", "scen_2", "pos"
 SCEN = (X, Z, C)
 SCEN_POS = (X, Z, C, Y)
 COLOURS = (((X, 0), (Z, 0), (Y, 0)), ((Z, 1), (Y, 1), (X, 0)), ((Y, 2), (X, 0), (Z, 0)))
+
+
+def to_column(row):
+    return jnp.broadcast_to(row, (LANES, LANES)).T
+
+
+def fill_starts(sizes_ref, col, books):
+    f32 = jnp.float32
+    sizes = sizes_ref[...].astype(f32)
+    down = lax.broadcasted_iota(jnp.int32, (LANES, LANES), 0)
+    across = lax.broadcasted_iota(jnp.int32, (LANES, LANES), 1)
+    upper = jnp.where(down <= across, 1.0, 0.0).astype(f32)
+    within = jnp.dot(sizes, upper, precision=lax.Precision.HIGHEST, preferred_element_type=f32)
+    before = [jnp.zeros((1, LANES), f32)]
+    for k in range(books // LANES - 1):
+        before.append(before[-1] + within[k : k + 1, LANES - 1 : LANES])
+    start = within - sizes + jnp.concatenate(before, axis=0)
+    for k in range(books // LANES):
+        col[LANES * k : LANES * (k + 1), :] = to_column(start[k : k + 1, :]).astype(jnp.int32)
+    col[books:, :] = jnp.full((col.shape[0] - books, LANES), 1 << 24, jnp.int32)
+
+
+def books_at(col, books, place):
+    count = jnp.zeros((8, LANES), jnp.int32)
+    for b in range(0, books, 8):
+        count = count + jnp.where(col[b : b + 8, :] <= place, 1, 0)
+    return jnp.sum(count, axis=0, keepdims=True) - 1
 
 
 def segsum_body(blocks, sizes_ref, x_hbm, out_ref, facts_ref, kept, col, sems):
@@ -28,19 +58,7 @@
         copies.append(pltpu.make_async_copy(x_hbm.at[:, piece], kept.at[:, piece], sems.at[n]))
         copies[-1].start()
 
-    exact = lax.Precision.HIGHEST
-    sizes = sizes_ref[...].astype(f32)
-    down = lax.broadcasted_iota(jnp.int32, (LANES, LANES), 0)
-    across = lax.broadcasted_iota(jnp.int32, (LANES, LANES), 1)
-    upper = jnp.where(down <= across, 1.0, 0.0).astype(f32)
-    within = jnp.dot(sizes, upper, precision=exact, preferred_element_type=f32)
-    before = [jnp.zeros((1, LANES), f32)]
-    for k in range(books // LANES - 1):
-        before.append(before[-1] + within[k : k + 1, LANES - 1 : LANES])
-    start = within - sizes + jnp.concatenate(before, axis=0)
-    for k in range(books // LANES):
-        col[LANES * k : LANES * (k + 1), :] = to_column(start[k : k + 1, :]).astype(jnp.int32)
-    col[books:, :] = jnp.full((col.shape[0] - books, LANES), 1 << 24, jnp.int32)
+    fill_starts(sizes_ref, col, books)
 
     lane = lax.broadcasted_iota(jnp.int32, (1, LANES), 1)
     place = jnp.zeros((1, LANES), jnp.int32)
@@ -50,19 +68,13 @@
     for j in range(4):
         place = jnp.where(lane == 32 + j, j * places, place)
         place = jnp.where(lane == 48 + j, j * places + places - 1, place)
-    count = jnp.zeros((8, LANES), jnp.int32)
-    for b in range(0, books, 8):
-        count = count + jnp.where(col[b : b + 8, :] <= place, 1, 0)
-    facts = jnp.sum(count, axis=0, keepdims=True) - 1
+    facts = books_at(col, books, place)
     facts = jnp.where((lane >= 32) & (lane < 48), facts // 8 * 8, facts)
 
     def fact(i):
-        return jnp.sum(jnp.where(lane == i, facts, 0).astype(f32)).astype(jnp.int32)
-
-    longest = fact(48) - fact(32)
-    for j in range(1, 4):
-        longest = jnp.maximum(longest, fact(48 + j) - fact(32 + j))
-    facts_ref[...] = jnp.where(lane == 64, longest, facts)
+        return jnp.sum(jnp.where(lane == i, facts, 0))
+
+    facts_ref[...] = facts
     mine = fact(32 + me)
     spans = [((fact(n) - mine) // TILE, (fact(16 + n) - mine) // TILE) for n in range(len(blocks))]
     out_ref[...] = jnp.zeros_like(out_ref)
@@ -120,15 +132,18 @@
     return high, (x - high.astype(jnp.float32)).astype(jnp.bfloat16)
 
 
-def to_column(row):
-    return jnp.broadcast_to(row, (LANES, LANES)).T
-
-
-def exchange_body(
-    cap, total, offs, owners, xc, cov, con,
-    owner, land, vsum, vland, yvec, z, full0, full1, own, gram, land1, land2, land3, part1, part2,
-    ysend, yrecv, vsend, vrecv, psend, precv, rsend, rrecv, osem,
-):
+def exchange_body(cap, total, fused, *refs):
+    if fused:
+        sizes, owners, x_hbm, cov, con, facts_ref = refs[:6]
+        kept, col, masks, sums_at, xc, csem = refs[6:12]
+        refs = refs[12:]
+    else:
+        offs, owners, xc, cov, con = refs[:5]
+        refs = refs[5:]
+    (
+        owner, land, vsum, xvec, yvec, z, full0, full1, own, gram, land1, land2, land3, part1, part2,
+        ysend, yrecv, vsend, vrecv, psend, precv, rsend, rrecv, osem,
+    ) = refs
     at = {name: lax.axis_index(name) for name in SCEN_POS}
     size = {X: 4, Z: 4, C: 2, Y: 4}
     full = (full0, full1)
@@ -139,8 +154,20 @@
 
     fetch = pltpu.make_async_copy(owners, owner, osem)
     fetch.start()
-    others = [{name: peer(name, p)} for name in SCEN_POS for p in range(1, size[name])]
-    others += [{C: peer(C, 1), Y: peer(Y, p)} for p in range(1, size[Y])]
+    around = [(a, b) for a in range(size[X]) for b in range(size[Z]) if a or b]
+    along = [(d, p) for p in (2, 1, 3, 0) for d in range(size[C]) if d or p]
+    others = [{X: peer(X, a), Z: peer(Z, b)} for a, b in around]
+    others += [{C: peer(C, d), Y: peer(Y, p)} for d, p in along]
+    if fused:
+        loads = []
+        for n, p in enumerate((2, 1, 3, 0)):
+            rows = pl.ds(pl.multiple_of(peer(Y, p) * LANES, LANES), LANES)
+            loads.append(
+                pltpu.make_async_copy(
+                    x_hbm.at[rows, :], kept.at[pl.ds(LANES * n, LANES), :], csem.at[n]
+                )
+            )
+            loads[-1].start()
     barrier = pltpu.get_barrier_semaphore()
     for other in others:
         pl.semaphore_signal(barrier, inc=1, device_id=other, device_id_type=pl.DeviceIdType.MESH)
@@ -162,57 +189,114 @@
         return send_to(src, dst, s, r, {name: peer(name, p)})
 
     started = []
+    zero = jnp.zeros((PAD, LANES), jnp.float32)
     chunks = []
-    for p in (2, 1, 3):
-        chunks.append(
-            send(
-                xc.at[peer(Y, p), pl.ds(0, cap), :], land.at[p - 1],
-                ysend.at[p - 1], yrecv.at[p - 1], Y, p,
-            )
+
+    def send_chunk(slot):
+        p = (2, 1, 3)[slot]
+        source = xc.at[slot] if fused else xc.at[peer(Y, p), pl.ds(0, cap), :]
+        chunks.append(send(source, land.at[p - 1], ysend.at[p - 1], yrecv.at[p - 1], Y, p))
+
+    if fused:
+        places = x_hbm.shape[1]
+        width = masks.shape[1] // sums_at.shape[1]
+        parts = places // width
+        fill_starts(sizes, col, books)
+        lane = lax.broadcasted_iota(jnp.int32, (1, LANES), 1)
+        blocks = 4 * parts
+        step = jnp.where(lane < blocks, width, places)
+        place = jnp.where(lane < blocks, lane, lane - blocks) * step
+        early = books_at(col, books, place) // 8 * 8
+        span = books_at(col, books, place + step - 1) - early
+        spare = jnp.where(
+            lane < blocks, WINDOW - 1 - span, jnp.where(lane < blocks + 4, cap - 1 - span, 0)
         )
+        facts_ref[...] = jnp.broadcast_to(jnp.min(spare, axis=1, keepdims=True), (1, LANES))
+
+        def fact(i):
+            return jnp.sum(jnp.where(lane == i, early, 0))
+
+        first = [fact(blocks + lax.rem(at[Y] + 4 - p, 4)) for p in range(4)]
+        begins = [fact(at[Y] * parts + i) for i in range(parts)]
+        lanes = lax.broadcasted_iota(jnp.int32, (WINDOW, LANES), 1)
+        for i in range(parts):
+            base = at[Y] * places + i * width
+            low = col[pl.ds(begins[i], WINDOW), :] - base
+            high = col[pl.ds(begins[i] + 1, WINDOW), :] - base
+            for l in range(0, width, LANES):
+                inside = (lanes + l >= low) & (lanes + l < high)
+                masks[:, i * width + l : i * width + l + LANES] = jnp.where(inside, 1.0, 0.0).astype(
+                    jnp.bfloat16
+                )
+            for q in range(4):
+                sums_at[q, i, 0:PAD, :] = zero
+                sums_at[q, i, PAD + WINDOW :, :] = zero
+        for a, b in GROUPS:
+            for q in range(a, b):
+                loads[q].wait()
+            for i in range(parts):
+                piece = slice(i * width, (i + 1) * width)
+                got = lax.dot_general(
+                    masks[:, piece], kept[LANES * a : LANES * b, piece],
+                    (((1,), (1,)), ((), ())), preferred_element_type=jnp.float32,
+                )
+                for q in range(a, b):
+                    sums_at[q, i, PAD : PAD + WINDOW, :] = got[:, LANES * (q - a) : LANES * (q - a + 1)]
+
+            def combine(t, carry):
+                for q in range(a, b):
+                    value = None
+                    for i in range(parts):
+                        u = lax.min(lax.max(t * PAD - (begins[i] - first[0]) + PAD, 0), WINDOW + PAD)
+                        got = sums_at[q, i, pl.ds(u, PAD), :]
+                        value = got if value is None else value + got
+                    xc[q, pl.ds(pl.multiple_of(t * PAD, PAD), PAD), :] = value
+                return carry
+
+            lax.fori_loop(0, cap // PAD, combine, 0, unroll=2)
+            for q in range(a, min(b, 3)):
+                send_chunk(q)
+    else:
+        first = [offs[0, 32 + lax.rem(at[Y] + 4 - p, 4)] for p in range(4)]
+        for q in range(3):
+            send_chunk(q)
 
     for b in range(0, cap, LANES):
         rows = slice(b, b + LANES)
         block = (xc[0, rows, :] + xc[1, rows, :]) + (xc[2, rows, :] + xc[3, rows, :])
-        vsum[0, :, rows] = block.T.reshape(LANES // 8, 8, LANES).sum(axis=0)
-    slot = 0
-    for stage, name in enumerate((X, Z)):
-        copies = []
-        for p in range(1, size[name]):
-            copies.append(
-                send(vsum.at[stage], vland.at[slot], vsend.at[slot], vrecv.at[slot], name, p)
-            )
-            slot += 1
-        value = vsum[stage]
-        for n, copy in enumerate(copies):
-            copy.wait_recv()
-            value = value + vland[slot - len(copies) + n]
-        vsum[stage + 1] = value
-        started += copies
+        vsum[0, :, rows] = block.T.sum(axis=0, keepdims=True)
+    xcopies = []
+    for n, (a, b) in enumerate(around):
+        xcopies.append(
+            send_to(vsum.at[0], xvec.at[n], vsend.at[n], vrecv.at[n], {X: peer(X, a), Z: peer(Z, b)})
+        )
+    value = vsum[0]
+    for n, copy in enumerate(xcopies):
+        copy.wait_recv()
+        value = value + xvec[n]
+    vsum[1] = value
+    started += xcopies
     ycopies = {}
-    for p in (2, 1, 3, 0):
-        for d in (0, 1):
-            if p or d:
-                ycopies[d, p] = send_to(
-                    vsum.at[2], yvec.at[4 * d + p], vsend.at[slot], vrecv.at[slot],
-                    {C: peer(C, d), Y: peer(Y, p)},
-                )
-                slot += 1
+    for n, (d, p) in enumerate(along):
+        slot = len(around) + n
+        ycopies[d, p] = send_to(
+            vsum.at[1], yvec.at[4 * d + p], vsend.at[slot], vrecv.at[slot],
+            {C: peer(C, d), Y: peer(Y, p)},
+        )
     started += ycopies.values()
 
-    zero = jnp.zeros((8, LANES), jnp.float32)
 
     def centre(p, values, sums):
-        z[p, 0:8, :] = zero
-        z[p, cap + 8 : cap + 16, :] = zero
-        mean = sums.sum(axis=0, keepdims=True) / total
+        z[p, 0:PAD, :] = zero
+        z[p, cap + PAD :, :] = zero
+        mean = sums / total
         for b in range(0, cap, LANES):
-            z[p, 8 + b : 8 + b + LANES, :] = values[b : b + LANES, :] - to_column(
+            z[p, PAD + b : PAD + b + LANES, :] = values[b : b + LANES, :] - to_column(
                 mean[:, b : b + LANES]
             )
 
     ycopies[1, 0].wait_recv()
-    centre(0, xc.at[at[Y]], vsum[2] + yvec[4])
+    centre(0, xc.at[3] if fused else xc.at[at[Y]], vsum[1] + yvec[4])
     for n, p in ((1, 1), (2, 3), (0, 2)):
         ycopies[0, p].wait_recv()
         ycopies[1, p].wait_recv()
@@ -220,19 +304,17 @@
         centre(p, land.at[p - 1], yvec[p] + yvec[4 + p])
     started += chunks
 
-    first = [offs[0, 32 + lax.rem(at[Y] + 4 - p, 4)] for p in range(4)]
-
     def put(t, carry):
-        row = t * 8
+        row = t * PAD
         value = None
         for p in range(4):
-            u = lax.min(lax.max(row - first[p] + 8, 0), cap + 8)
-            got = z[p, pl.ds(u, 8), :]
+            u = lax.min(lax.max(row - first[p] + PAD, 0), cap + PAD)
+            got = z[p, pl.ds(u, PAD), :]
             value = got if value is None else value + got
-        full0[pl.ds(pl.multiple_of(row, 8), 8), :] = value
+        full0[pl.ds(pl.multiple_of(row, PAD), PAD), :] = value
         return carry
 
-    lax.fori_loop(0, books // 8, put, 0, unroll=8)
+    lax.fori_loop(0, books // PAD, put, 0, unroll=2)
     pair = send(full0, full1, psend, precv, C, 1)
     started.append(pair)
 
@@ -317,31 +399,50 @@
         copy.wait_send()
 
 
-def exchange(xc, facts, owner, cap, total, collective):
-    books = xc.shape[1]
+def exchange(operands, owner, cap, total, collective, fused):
+    books = owner.shape[0]
     f32 = jnp.float32
     pieces = books // LANES + 1
     rows = books // 128
     dma = pltpu.SemaphoreType.DMA
+    out_shape = [
+        jax.ShapeDtypeStruct((rows, books), f32),
+        jax.ShapeDtypeStruct((rows, LANES), f32),
+    ]
+    vmem = pl.BlockSpec(memory_space=pltpu.VMEM)
+    hbm = pl.BlockSpec(memory_space=pl.ANY)
+    if fused:
+        sizes, losses = operands
+        operands = (sizes.reshape(books // LANES, LANES), owner, losses)
+        in_specs = [vmem, hbm, hbm]
+        out_shape.append(jax.ShapeDtypeStruct((1, LANES), jnp.int32))
+        places = losses.shape[1]
+        parts = places // 2048
+        scratch = [
+            pltpu.VMEM(losses.shape, losses.dtype),
+            pltpu.VMEM((books + 2 * LANES, LANES), jnp.int32),
+            pltpu.VMEM((WINDOW, places), losses.dtype),
+            pltpu.VMEM((4, parts, WINDOW + 2 * PAD, LANES), f32),
+            pltpu.VMEM((4, cap, LANES), f32),
+            dma((4,)),
+        ]
+    else:
+        facts, xc = operands
+        operands = (facts, owner, xc)
+        in_specs = [pl.BlockSpec(memory_space=pltpu.SMEM), hbm, vmem]
+        scratch = []
     return pl.pallas_call(
-        functools.partial(exchange_body, cap, total),
-        out_shape=(
-            jax.ShapeDtypeStruct((rows, books), f32),
-            jax.ShapeDtypeStruct((rows, LANES), f32),
-        ),
-        in_specs=[
-            pl.BlockSpec(memory_space=pltpu.SMEM),
-            pl.BlockSpec(memory_space=pl.ANY),
-            pl.BlockSpec(memory_space=pltpu.VMEM),
-        ],
-        out_specs=[pl.BlockSpec(memory_space=pltpu.VMEM)] * 2,
-        scratch_shapes=[
+        functools.partial(exchange_body, cap, total, fused),
+        out_shape=out_shape,
+        in_specs=in_specs,
+        out_specs=[vmem] * len(out_shape),
+        scratch_shapes=scratch + [
             pltpu.SMEM(owner.shape, jnp.int32),
             pltpu.VMEM((3, cap, LANES), f32),
-            pltpu.VMEM((3, 8, cap), f32),
-            pltpu.VMEM((6, 8, cap), f32),
-            pltpu.VMEM((8, 8, cap), f32),
-            pltpu.VMEM((4, cap + 16, LANES), f32),
+            pltpu.VMEM((2, 1, cap), f32),
+            pltpu.VMEM((15, 1, cap), f32),
+            pltpu.VMEM((8, 1, cap), f32),
+            pltpu.VMEM((4, cap + 2 * PAD, LANES), f32),
             pltpu.VMEM((books, LANES), f32),
             pltpu.VMEM((books, LANES), f32),
             pltpu.VMEM((2, books // 2, LANES), f32),
@@ -351,27 +452,31 @@
             pltpu.VMEM((pieces, 3, 8, LANES), f32),
             pltpu.VMEM((pieces, 4, 4, 8, LANES), f32),
             pltpu.VMEM((pieces, 4, 8, LANES), f32),
-            dma((3,)), dma((3,)), dma((13,)), dma((13,)), dma, dma,
+            dma((3,)), dma((3,)), dma((22,)), dma((22,)), dma, dma,
             dma((3, pieces, 3)), dma((3, pieces, 3)), dma,
         ],
         name="exchange_%d" % cap,
         compiler_params=pltpu.CompilerParams(
-            collective_id=collective, has_side_effects=True, vmem_limit_bytes=40 << 20
+            collective_id=collective, has_side_effects=True, vmem_limit_bytes=56 << 20
         ),
-    )(facts, owner, xc)
+    )(*operands)
 
 
 def per_device(losses, book_sizes, owner_books):
     rows, places = losses.shape
     books = book_sizes.shape[0]
     total = rows * lax.axis_size(SCEN)
-    xc, facts = segment_sums(losses, book_sizes)
-    fits = facts[0, 64] < SHORT
+    cov, con, spare = exchange((book_sizes, losses), owner_books, SHORT, total, 1, True)
+
+    def general(cov, con, losses, sizes, owner):
+        xc, facts = segment_sums(losses, sizes)
+        return tuple(exchange((facts, xc), owner, books, total, 2, False))
+
     cov, con = lax.cond(
-        fits,
-        lambda *a: exchange(*a, SHORT, total, 1),
-        lambda *a: exchange(*a, books, total, 2),
-        xc, facts, owner_books,
+        spare[0, 0] >= 0,
+        lambda cov, con, *rest: (cov, con),
+        general,
+        cov, con, losses, book_sizes, owner_books,
     )
     return cov, con[:, 0]
 

time: 57.5 us -> 54.5 us (0.948)
  Pallas kernels: 53.6 us -> 52.2 us
  local copies, waits for them, and re-layouts: 2 us -> 0.74 us
    pallas_call x2 -> x1, Pallas kernels: 53.6 us -> 52.2 us  [exchange(): pl.pallas_call(functools.partial(exchange_body, cap, total, fused), out_s...]
    unnamed x7, local copies, waits for them, and re-layouts: 1.3 us -> 0.63 us
    slice x1 -> x0, local copies, waits for them, and re-layouts: 0.58 us -> none  [per_device(): fits = facts[0, 64] < SHORT]
where the time goes in v4:
time: 54.5 us; the launch traced here: 54.4 us
  Pallas kernels  52.2 us (96%)
  between operations  1.23 us (2%)
  local copies, waits for them, and re-layouts  0.74 us (1%)
    pallas_call x1, Pallas kernels, exchange(): pl.pallas_call(functools.partial(exchange_body, cap, total, fused), out_s...  52.2 us

profile of v4, /device:TPU:0, one launch (start us, length us, event | category | flops | bytes accessed | tf_op | source)
XLA Modules:
  0.0 54.4 jit_solution(17610877958940934918)
XLA Ops:
  0.6 0.0 copy-start.3
  0.6 0.0 copy-start.2
  0.6 52.2 %exchange_384.1 = (f32[8,1024]{1,0:T(8,128)S(1)}, f32[8,128]{1,0:T(8,128)S(1)}, s32[1,128]{1,0:T(1,128)}) custom-call(s32[8,128]{1,0:T(8,128)} %bitcast.4, s32[1024]{0:T(1024)} %refs_1_.1, bf16[512,16384]{1,0:T(8,128)(2,1)} %refs_2_.1), custom_call_target="tpu_custom_call" | custom-call | tf_op jit(solution)/shard_map/exchange_384/pallas_call | solution.py:434
  53.4 0.0 copy-done.3
  53.4 0.0 copy-done.2
  53.4 0.4 conditional.1
  53.7 0.1 slice_reduce_fusion.1
  53.8 0.0 copy-start.4
  53.8 0.6 %copy.10 = f32[8,1024]{1,0:T(8,128)} copy(f32[8,1024]{1,0:T(8,128)S(1)} %get-tuple-element.43) | data formatting | bytes 65536
  54.4 0.0 copy-done.4
Async XLA Ops:
  0.6 52.8 %copy-start.3 = (s32[1024]{0:T(1024)S(1)}, s32[1024]{0:T(1024)}, u32[]{:S(2)}) copy-start(s32[1024]{0:T(1024)} %refs_1_.1) | copy-start | bytes 12292
  0.6 52.8 %copy-start.2 = (s32[1024]{0:T(1024)S(1)}, s32[1024]{0:T(1024)}, u32[]{:S(2)}) copy-start(s32[1024]{0:T(1024)} %param.6) | copy-start | bytes 12292
  53.8 0.6 %copy-start.4 = (f32[8]{0:T(128)}, f32[8]{0:T(128)S(1)}, u32[]{:S(2)}) copy-start(f32[8]{0:T(128)S(1)} %get-tuple-element.44) | copy-start | bytes 100

commit v5 on v4

--- a/solution.py
+++ b/solution.py
@@ -141,8 +141,8 @@
         offs, owners, xc, cov, con = refs[:5]
         refs = refs[5:]
     (
-        owner, land, vsum, xvec, yvec, z, full0, full1, own, gram, land1, land2, land3, part1, part2,
-        ysend, yrecv, vsend, vrecv, psend, precv, rsend, rrecv, osem,
+        owner, land, vsum, xvec, yvec, z, zmean, full0, full1, mean, own, gram, relay, land1, land2, land3,
+        part1, part2, ysend, yrecv, vsend, vrecv, psend, precv, esend, erecv, rsend, rrecv, osem,
     ) = refs
     at = {name: lax.axis_index(name) for name in SCEN_POS}
     size = {X: 4, Z: 4, C: 2, Y: 4}
@@ -219,15 +219,18 @@
         first = [fact(blocks + lax.rem(at[Y] + 4 - p, 4)) for p in range(4)]
         begins = [fact(at[Y] * parts + i) for i in range(parts)]
         lanes = lax.broadcasted_iota(jnp.int32, (WINDOW, LANES), 1)
-        for i in range(parts):
+
+        def member(i):
             base = at[Y] * places + i * width
             low = col[pl.ds(begins[i], WINDOW), :] - base
             high = col[pl.ds(begins[i] + 1, WINDOW), :] - base
+            tiles = []
             for l in range(0, width, LANES):
                 inside = (lanes + l >= low) & (lanes + l < high)
-                masks[:, i * width + l : i * width + l + LANES] = jnp.where(inside, 1.0, 0.0).astype(
-                    jnp.bfloat16
-                )
+                tiles.append(jnp.where(inside, 1.0, 0.0).astype(jnp.bfloat16))
+            return jnp.concatenate(tiles, axis=1)
+
+        for i in range(parts):
             for q in range(4):
                 sums_at[q, i, 0:PAD, :] = zero
                 sums_at[q, i, PAD + WINDOW :, :] = zero
@@ -236,8 +239,13 @@
                 loads[q].wait()
             for i in range(parts):
                 piece = slice(i * width, (i + 1) * width)
+                if a == 0:
+                    chosen = member(i)
+                    masks[:, piece] = chosen
+                else:
+                    chosen = masks[:, piece]
                 got = lax.dot_general(
-                    masks[:, piece], kept[LANES * a : LANES * b, piece],
+                    chosen, kept[LANES * a : LANES * b, piece],
                     (((1,), (1,)), ((), ())), preferred_element_type=jnp.float32,
                 )
                 for q in range(a, b):
@@ -286,63 +294,105 @@
     started += ycopies.values()
 
 
-    def centre(p, values, sums):
-        z[p, 0:PAD, :] = zero
-        z[p, cap + PAD :, :] = zero
-        mean = sums / total
-        for b in range(0, cap, LANES):
-            z[p, PAD + b : PAD + b + LANES, :] = values[b : b + LANES, :] - to_column(
-                mean[:, b : b + LANES]
-            )
-
-    ycopies[1, 0].wait_recv()
-    centre(0, xc.at[3] if fused else xc.at[at[Y]], vsum[1] + yvec[4])
-    for n, p in ((1, 1), (2, 3), (0, 2)):
-        ycopies[0, p].wait_recv()
-        ycopies[1, p].wait_recv()
-        chunks[n].wait_recv()
-        centre(p, land.at[p - 1], yvec[p] + yvec[4 + p])
+    for p in range(4):
+        for ref in (z, zmean):
+            ref[p, 0:PAD, :] = zero
+            ref[p, cap + PAD :, :] = zero
+    z[0, PAD : PAD + cap, :] = xc[3] if fused else xc[at[Y], 0:cap, :]
+    for copy, p in zip(chunks, (2, 1, 3)):
+        copy.wait_recv()
+        z[p, PAD : PAD + cap, :] = land[p - 1]
     started += chunks
 
-    def put(t, carry):
-        row = t * PAD
-        value = None
-        for p in range(4):
-            u = lax.min(lax.max(row - first[p] + PAD, 0), cap + PAD)
-            got = z[p, pl.ds(u, PAD), :]
-            value = got if value is None else value + got
-        full0[pl.ds(pl.multiple_of(row, PAD), PAD), :] = value
-        return carry
-
-    lax.fori_loop(0, books // PAD, put, 0, unroll=2)
+    def place_books(source, target):
+        def put(t, carry):
+            row = t * PAD
+            value = None
+            for p in range(4):
+                u = lax.min(lax.max(row - first[p] + PAD, 0), cap + PAD)
+                got = source[p, pl.ds(u, PAD), :]
+                value = got if value is None else value + got
+            target[pl.ds(pl.multiple_of(row, PAD), PAD), :] = value
+            return carry
+
+        lax.fori_loop(0, books // PAD, put, 0, unroll=2)
+
+    place_books(z, full0)
     pair = send(full0, full1, psend, precv, C, 1)
     started.append(pair)
 
     core = at[C]
 
-    def gather(h):
+    def gather(source, h):
         def some(g, carry):
             k0 = (g // 4) * 64 + core * 32 + lax.rem(g, 4) * 8
             for r in range(8):
                 book = owner[k0 + r]
-                own[h, pl.ds(g * 8 + r, 1), :] = full[h][pl.ds(book, 1), :]
+                own[h, pl.ds(g * 8 + r, 1), :] = source[pl.ds(book, 1), :]
             return carry
 
         lax.fori_loop(0, own.shape[1] // 8, some, 0, unroll=2)
 
     fetch.wait()
-    gather(0)
+    gather(full0, 0)
+
+    for p in range(4):
+        sums = vsum[1] if p == 0 else None
+        for d in (0, 1):
+            if d or p:
+                ycopies[d, p].wait_recv()
+                sums = yvec[4 * d + p] if sums is None else sums + yvec[4 * d + p]
+        average = sums / total
+        for b in range(0, cap, LANES):
+            zmean[p, PAD + b : PAD + b + LANES, :] = to_column(average[:, b : b + LANES])
+    place_books(zmean, mean)
+    gather(mean, 2)
     pair.wait_recv()
-    gather(1)
-
-    sums = [full[h][...].reshape(books // 8, 8, LANES).sum(axis=0).sum(axis=0, keepdims=True) for h in (0, 1)]
-    square = (sums[0] * sums[0] + sums[1] * sums[1]).sum(axis=1, keepdims=True)
+    gather(full1, 1)
+
     pieces = books // LANES + 1
     each = pieces // 3
-    gram[pieces - 1] = jnp.broadcast_to(square, (4, 4, 4, 8, LANES))
 
     def pick(ref, dim, index):
         return ref.at[(slice(None),) * dim + (index,)]
+
+    def half(n, index, h):
+        dim = COLOURS[n // each][0][1]
+        some = pl.ds(2 * h, 2)
+        where = [(index, some), (some, index), (some, slice(None), index)][dim]
+        return gram.at[(n, *where)]
+
+    def first_out(n):
+        name = COLOURS[n // each][0][0]
+        ahead, behind = peer(name, 1), peer(name, 3)
+        copies = []
+        for k, (index, h, target, p) in enumerate((
+            (peer(name, 2), 0, relay.at[n, 0], 1),
+            (peer(name, 2), 1, relay.at[n, 1], 3),
+            (ahead, 1, land1.at[n, 0, pl.ds(2, 2)], 1),
+            (behind, 0, land1.at[n, 1, pl.ds(0, 2)], 3),
+        )):
+            copies.append(send(half(n, index, h), target, esend.at[n, k], erecv.at[n, k], name, p))
+        return copies
+
+    def first_relay(n, copies):
+        name = COLOURS[n // each][0][0]
+        for h, p in ((0, 1), (1, 3)):
+            copies[h].wait_recv()
+            relay[n, h] = relay[n, h] + half(n, peer(name, p), h)[...]
+            copies.append(
+                send(
+                    relay.at[n, h], land1.at[n, h, pl.ds(2 * h, 2)],
+                    esend.at[n, 4 + h], erecv.at[n, 4 + h], name, p,
+                )
+            )
+
+    def first_sum(n, copies):
+        name, dim = COLOURS[n // each][0]
+        for copy in copies[2:]:
+            copy.wait_recv()
+        started.extend(copies)
+        return pick(gram.at[n], dim, at[name])[...] + (land1[n, 0] + land1[n, 1])
 
     def scatter(stage, n, source, lands):
         name, dim = COLOURS[n // each][stage]
@@ -351,7 +401,7 @@
             copies.append(
                 (p, send(
                     pick(source, dim, peer(name, p)), lands.at[n, p - 1],
-                    rsend.at[stage, n, p - 1], rrecv.at[stage, n, p - 1], name, p,
+                    rsend.at[stage - 1, n, p - 1], rrecv.at[stage - 1, n, p - 1], name, p,
                 ))
             )
         return copies
@@ -367,22 +417,32 @@
 
     order = [each * c + q for q in range(each) for c in range(3)]
     flying = {}
-    a0h, a0l = split(own[0])
-    a1h, a1l = split(own[1])
+    a0h, a0l = split(own[0] - own[2])
+    a1h, a1l = split(own[1] - own[2])
     left = jnp.concatenate([a0h, a1h, a0h, a1h, a0l, a1l], axis=1)
     for n in order:
         if n < pieces - 1:
             rows = slice(LANES * n, LANES * (n + 1))
-            b0h, b0l = split(full0[rows, :])
-            b1h, b1l = split(full1[rows, :])
+            b0h, b0l = split(full0[rows, :] - mean[rows, :])
+            b1h, b1l = split(full1[rows, :] - mean[rows, :])
             right = jnp.concatenate([b0h, b1h, b0l, b1l, b0h, b1h], axis=1)
             got = lax.dot_general(
                 left, right, (((1,), (1,)), ((), ())), preferred_element_type=jnp.float32
             )
             gram[n] = got.reshape(4, 4, 4, 8, LANES)
-        flying[n] = scatter(0, n, gram.at[n], land1)
+        else:
+            square = None
+            for ref in (full0, full1):
+                whole = (ref[...] - mean[...]).reshape(books // 8, 8, LANES).sum(axis=0)
+                whole = whole.sum(axis=0, keepdims=True)
+                square = whole * whole if square is None else square + whole * whole
+            square = square.sum(axis=1, keepdims=True)
+            gram[n] = jnp.broadcast_to(square, (4, 4, 4, 8, LANES))
+        flying[n] = first_out(n)
     for n in order:
-        part1[n] = reduce(0, n, gram.at[n], land1, flying[n])
+        first_relay(n, flying[n])
+    for n in order:
+        part1[n] = first_sum(n, flying[n])
         flying[n] = scatter(1, n, part1.at[n], land2)
     for n in order:
         part2[n] = reduce(1, n, part1.at[n], land2, flying[n])
@@ -443,17 +503,20 @@
             pltpu.VMEM((15, 1, cap), f32),
             pltpu.VMEM((8, 1, cap), f32),
             pltpu.VMEM((4, cap + 2 * PAD, LANES), f32),
+            pltpu.VMEM((4, cap + 2 * PAD, LANES), f32),
             pltpu.VMEM((books, LANES), f32),
             pltpu.VMEM((books, LANES), f32),
-            pltpu.VMEM((2, books // 2, LANES), f32),
+            pltpu.VMEM((books, LANES), f32),
+            pltpu.VMEM((3, books // 2, LANES), f32),
             pltpu.VMEM((pieces, 4, 4, 4, 8, LANES), f32),
-            pltpu.VMEM((pieces, 3, 4, 4, 8, LANES), f32),
+            pltpu.VMEM((pieces, 2, 2, 4, 8, LANES), f32),
+            pltpu.VMEM((pieces, 2, 4, 4, 8, LANES), f32),
             pltpu.VMEM((pieces, 3, 4, 8, LANES), f32),
             pltpu.VMEM((pieces, 3, 8, LANES), f32),
             pltpu.VMEM((pieces, 4, 4, 8, LANES), f32),
             pltpu.VMEM((pieces, 4, 8, LANES), f32),
             dma((3,)), dma((3,)), dma((22,)), dma((22,)), dma, dma,
-            dma((3, pieces, 3)), dma((3, pieces, 3)), dma,
+            dma((pieces, 6)), dma((pieces, 6)), dma((2, pieces, 3)), dma((2, pieces, 3)), dma,
         ],
         name="exchange_%d" % cap,
         compiler_params=pltpu.CompilerParams(

time: 54.5 us -> 52.1 us (0.956)
  Pallas kernels: 52.2 us -> 49.8 us
    pallas_call x1, Pallas kernels: 52.2 us -> 49.8 us  [exchange(): pl.pallas_call(functools.partial(exchange_body, cap, total, fused), out_s...]
where the time goes in v5:
time: 52.1 us; the launch traced here: 52 us
  Pallas kernels  49.8 us (96%)
  between operations  1.23 us (2%)
  local copies, waits for them, and re-layouts  0.74 us (1%)
    pallas_call x1, Pallas kernels, exchange(): pl.pallas_call(functools.partial(exchange_body, cap, total, fused), out_s...  49.8 us

profile of v5, /device:TPU:0, one launch (start us, length us, event | category | flops | bytes accessed | tf_op | source)
XLA Modules:
  0.0 52.0 jit_solution(17402918094382850057)
XLA Ops:
  0.6 0.0 copy-start.3
  0.6 0.0 copy-start.2
  0.6 49.8 %exchange_384.1 = (f32[8,1024]{1,0:T(8,128)S(1)}, f32[8,128]{1,0:T(8,128)S(1)}, s32[1,128]{1,0:T(1,128)}) custom-call(s32[8,128]{1,0:T(8,128)} %bitcast.4, s32[1024]{0:T(1024)} %refs_1_.1, bf16[512,16384]{1,0:T(8,128)(2,1)} %refs_2_.1), custom_call_target="tpu_custom_call" | custom-call | tf_op jit(solution)/shard_map/exchange_384/pallas_call | solution.py:494
  51.0 0.0 copy-done.3
  51.0 0.0 copy-done.2
  51.0 0.4 conditional.1
  51.3 0.1 slice_reduce_fusion.1
  51.4 0.0 copy-start.4
  51.4 0.6 %copy.10 = f32[8,1024]{1,0:T(8,128)} copy(f32[8,1024]{1,0:T(8,128)S(1)} %get-tuple-element.43) | data formatting | bytes 65536
  52.0 0.0 copy-done.4
Async XLA Ops:
  0.6 50.4 %copy-start.3 = (s32[1024]{0:T(1024)S(1)}, s32[1024]{0:T(1024)}, u32[]{:S(2)}) copy-start(s32[1024]{0:T(1024)} %refs_1_.1) | copy-start | bytes 12292
  0.6 50.4 %copy-start.2 = (s32[1024]{0:T(1024)S(1)}, s32[1024]{0:T(1024)}, u32[]{:S(2)}) copy-start(s32[1024]{0:T(1024)} %param.6) | copy-start | bytes 12292
  51.4 0.6 %copy-start.4 = (f32[8]{0:T(128)}, f32[8]{0:T(128)S(1)}, u32[]{:S(2)}) copy-start(f32[8]{0:T(128)S(1)} %get-tuple-element.44) | copy-start | bytes 100

commit v6 on v5

--- a/solution.py
+++ b/solution.py
@@ -171,7 +171,8 @@
     barrier = pltpu.get_barrier_semaphore()
     for other in others:
         pl.semaphore_signal(barrier, inc=1, device_id=other, device_id_type=pl.DeviceIdType.MESH)
-    pl.semaphore_wait(barrier, len(others))
+    if not fused:
+        pl.semaphore_wait(barrier, len(others))
 
     def send_to(src, dst, s, r, device):
         copy = pltpu.make_async_remote_copy(
@@ -262,6 +263,8 @@
                 return carry
 
             lax.fori_loop(0, cap // PAD, combine, 0, unroll=2)
+            if a == 0:
+                pl.semaphore_wait(barrier, len(others))
             for q in range(a, min(b, 3)):
                 send_chunk(q)
     else:
@@ -420,16 +423,21 @@
     a0h, a0l = split(own[0] - own[2])
     a1h, a1l = split(own[1] - own[2])
     left = jnp.concatenate([a0h, a1h, a0h, a1h, a0l, a1l], axis=1)
-    for n in order:
-        if n < pieces - 1:
-            rows = slice(LANES * n, LANES * (n + 1))
-            b0h, b0l = split(full0[rows, :] - mean[rows, :])
-            b1h, b1l = split(full1[rows, :] - mean[rows, :])
-            right = jnp.concatenate([b0h, b1h, b0l, b1l, b0h, b1h], axis=1)
+    for k in range(0, pieces, 2):
+        pair = order[k : k + 2]
+        if k < pieces - 1:
+            right = []
+            for n in pair:
+                rows = slice(LANES * n, LANES * (n + 1))
+                b0h, b0l = split(full0[rows, :] - mean[rows, :])
+                b1h, b1l = split(full1[rows, :] - mean[rows, :])
+                right.append(jnp.concatenate([b0h, b1h, b0l, b1l, b0h, b1h], axis=1))
             got = lax.dot_general(
-                left, right, (((1,), (1,)), ((), ())), preferred_element_type=jnp.float32
+                left, jnp.concatenate(right, axis=0), (((1,), (1,)), ((), ())),
+                preferred_element_type=jnp.float32,
             )
-            gram[n] = got.reshape(4, 4, 4, 8, LANES)
+            for m, n in enumerate(pair):
+                gram[n] = got[:, LANES * m : LANES * (m + 1)].reshape(4, 4, 4, 8, LANES)
         else:
             square = None
             for ref in (full0, full1):
@@ -437,8 +445,9 @@
                 whole = whole.sum(axis=0, keepdims=True)
                 square = whole * whole if square is None else square + whole * whole
             square = square.sum(axis=1, keepdims=True)
-            gram[n] = jnp.broadcast_to(square, (4, 4, 4, 8, LANES))
-        flying[n] = first_out(n)
+            gram[pieces - 1] = jnp.broadcast_to(square, (4, 4, 4, 8, LANES))
+        for n in pair:
+            flying[n] = first_out(n)
     for n in order:
         first_relay(n, flying[n])
     for n in order:

time: 52.1 us -> 49.1 us (0.942)
  Pallas kernels: 49.8 us -> 46.7 us
    pallas_call x1, Pallas kernels: 49.8 us -> 46.7 us  [exchange(): pl.pallas_call(functools.partial(exchange_body, cap, total, fused), out_s...]
where the time goes in v6:
time: 49.1 us; the launch traced here: 48.9 us
  Pallas kernels  46.7 us (95%)
  between operations  1.23 us (3%)
  local copies, waits for them, and re-layouts  0.74 us (2%)
    pallas_call x1, Pallas kernels, exchange(): pl.pallas_call(functools.partial(exchange_body, cap, total, fused), out_s...  46.7 us

profile of v6, /device:TPU:0, one launch (start us, length us, event | category | flops | bytes accessed | tf_op | source)
XLA Modules:
  0.0 48.9 jit_solution(11870959909831470107)
XLA Ops:
  0.6 0.0 copy-start.3
  0.6 0.0 copy-start.2
  0.6 46.7 %exchange_384.1 = (f32[8,1024]{1,0:T(8,128)S(1)}, f32[8,128]{1,0:T(8,128)S(1)}, s32[1,128]{1,0:T(1,128)}) custom-call(s32[8,128]{1,0:T(8,128)} %bitcast.4, s32[1024]{0:T(1024)} %refs_1_.1, bf16[512,16384]{1,0:T(8,128)(2,1)} %refs_2_.1), custom_call_target="tpu_custom_call" | custom-call | tf_op jit(solution)/shard_map/exchange_384/pallas_call | solution.py:503
  47.9 0.0 copy-done.3
  47.9 0.0 copy-done.2
  47.9 0.4 conditional.1
  48.2 0.1 slice_reduce_fusion.1
  48.3 0.0 copy-start.4
  48.3 0.6 %copy.10 = f32[8,1024]{1,0:T(8,128)} copy(f32[8,1024]{1,0:T(8,128)S(1)} %get-tuple-element.43) | data formatting | bytes 65536
  48.9 0.0 copy-done.4
Async XLA Ops:
  0.6 47.3 %copy-start.3 = (s32[1024]{0:T(1024)S(1)}, s32[1024]{0:T(1024)}, u32[]{:S(2)}) copy-start(s32[1024]{0:T(1024)} %refs_1_.1) | copy-start | bytes 12292
  0.6 47.3 %copy-start.2 = (s32[1024]{0:T(1024)S(1)}, s32[1024]{0:T(1024)}, u32[]{:S(2)}) copy-start(s32[1024]{0:T(1024)} %param.6) | copy-start | bytes 12292
  48.3 0.6 %copy-start.4 = (f32[8]{0:T(128)}, f32[8]{0:T(128)S(1)}, u32[]{:S(2)}) copy-start(f32[8]{0:T(128)S(1)} %get-tuple-element.44) | copy-start | bytes 100

commit v7 on v6

--- a/solution.py
+++ b/solution.py
@@ -41,10 +41,11 @@
 
 
 def books_at(col, books, place):
-    count = jnp.zeros((8, LANES), jnp.int32)
+    counts = [jnp.zeros((8, LANES), jnp.int32) for _ in range(8)]
     for b in range(0, books, 8):
-        count = count + jnp.where(col[b : b + 8, :] <= place, 1, 0)
-    return jnp.sum(count, axis=0, keepdims=True) - 1
+        k = b // 8 % 8
+        counts[k] = counts[k] + jnp.where(col[b : b + 8, :] <= place, 1, 0)
+    return jnp.sum(sum(counts), axis=0, keepdims=True) - 1
 
 
 def segsum_body(blocks, sizes_ref, x_hbm, out_ref, facts_ref, kept, col, sems):
@@ -262,7 +263,7 @@
                     xc[q, pl.ds(pl.multiple_of(t * PAD, PAD), PAD), :] = value
                 return carry
 
-            lax.fori_loop(0, cap // PAD, combine, 0, unroll=2)
+            lax.fori_loop(0, cap // PAD, combine, 0, unroll=4)
             if a == 0:
                 pl.semaphore_wait(barrier, len(others))
             for q in range(a, min(b, 3)):
@@ -318,7 +319,7 @@
             target[pl.ds(pl.multiple_of(row, PAD), PAD), :] = value
             return carry
 
-        lax.fori_loop(0, books // PAD, put, 0, unroll=2)
+        lax.fori_loop(0, books // PAD, put, 0, unroll=8)
 
     place_books(z, full0)
     pair = send(full0, full1, psend, precv, C, 1)
@@ -334,7 +335,7 @@
                 own[h, pl.ds(g * 8 + r, 1), :] = source[pl.ds(book, 1), :]
             return carry
 
-        lax.fori_loop(0, own.shape[1] // 8, some, 0, unroll=2)
+        lax.fori_loop(0, own.shape[1] // 8, some, 0, unroll=8)
 
     fetch.wait()
     gather(full0, 0)

time: 49.1 us -> 48.5 us (0.988)
  Pallas kernels: 46.7 us -> 46.1 us
    pallas_call x1, Pallas kernels: 46.7 us -> 46.1 us  [exchange(): pl.pallas_call(functools.partial(exchange_body, cap, total, fused), out_s...]
where the time goes in v7:
time: 48.5 us; the launch traced here: 48.4 us
  Pallas kernels  46.1 us (95%)
  between operations  1.23 us (3%)
  local copies, waits for them, and re-layouts  0.74 us (2%)
    pallas_call x1, Pallas kernels, exchange(): pl.pallas_call(functools.partial(exchange_body, cap, total, fused), out_s...  46.1 us

profile of v7, /device:TPU:0, one launch (start us, length us, event | category | flops | bytes accessed | tf_op | source)
XLA Modules:
  0.0 48.4 jit_solution(3335038813698125462)
XLA Ops:
  0.6 0.0 copy-start.3
  0.6 0.0 copy-start.2
  0.6 46.1 %exchange_384.1 = (f32[8,1024]{1,0:T(8,128)S(1)}, f32[8,128]{1,0:T(8,128)S(1)}, s32[1,128]{1,0:T(1,128)}) custom-call(s32[8,128]{1,0:T(8,128)} %bitcast.4, s32[1024]{0:T(1024)} %refs_1_.1, bf16[512,16384]{1,0:T(8,128)(2,1)} %refs_2_.1), custom_call_target="tpu_custom_call" | custom-call | tf_op jit(solution)/shard_map/exchange_384/pallas_call | solution.py:504
  47.3 0.0 copy-done.3
  47.4 0.0 copy-done.2
  47.4 0.4 conditional.1
  47.6 0.1 slice_reduce_fusion.1
  47.7 0.0 copy-start.4
  47.7 0.6 %copy.10 = f32[8,1024]{1,0:T(8,128)} copy(f32[8,1024]{1,0:T(8,128)S(1)} %get-tuple-element.43) | data formatting | bytes 65536
  48.3 0.0 copy-done.4
Async XLA Ops:
  0.6 46.7 %copy-start.3 = (s32[1024]{0:T(1024)S(1)}, s32[1024]{0:T(1024)}, u32[]{:S(2)}) copy-start(s32[1024]{0:T(1024)} %refs_1_.1) | copy-start | bytes 12292
  0.6 46.7 %copy-start.2 = (s32[1024]{0:T(1024)S(1)}, s32[1024]{0:T(1024)}, u32[]{:S(2)}) copy-start(s32[1024]{0:T(1024)} %param.6) | copy-start | bytes 12292
  47.7 0.6 %copy-start.4 = (f32[8]{0:T(128)}, f32[8]{0:T(128)S(1)}, u32[]{:S(2)}) copy-start(f32[8]{0:T(128)S(1)} %get-tuple-element.44) | copy-start | bytes 100
